TPU v7x, 32 devices: a whole 2x2x4 slice. The times are simulated.
32 devices in a mesh: dp: 16 (over z, y, core), tensor: 2 (over x).
Axes of the slice: x: 2, y: 2, z: 4, core: 2. Of those that a mesh axis runs over, the one named last changes fastest.
Arguments:
- tokens: bfloat16 [32768, 1024], P(('dp', 'tensor')), may hold values from -6 to 6
- gain_one: float32 [1024], replicated, may hold values from 0.5 to 1.5
- gain_two: float32 [1024], replicated, may hold values from 0.5 to 1.5
- w_query: bfloat16 [1024, 1024], P(None, 'tensor'), may hold values from -0.1875 to 0.1875
- w_key: bfloat16 [512, 1024], P('tensor'), may hold values from -0.1875 to 0.1875
- w_value: bfloat16 [512, 1024], P('tensor'), may hold values from -0.1875 to 0.1875
- w_out: bfloat16 [1024, 1024], P('tensor'), may hold values from -1 to 1
- w_gate: bfloat16 [32, 512, 1024], P(None, 'tensor'), may hold values from -0.1875 to 0.1875
- w_up: bfloat16 [32, 512, 1024], P(None, 'tensor'), may hold values from -0.1875 to 0.1875
- w_down: bfloat16 [32, 512, 1024], P(None, 'tensor'), may hold values from -1 to 1
- slot_index: int32 [16, 32, 640], P('dp'), may hold values from 0 to 2047, as said below
- slot_gate: float32 [16, 32, 640], P('dp'), may hold values from 0 to 0.19, as said below
- grad_output: bfloat16 [32768, 1024], P(('dp', 'tensor')), may hold values from -6 to 6
Outputs:
- output: bfloat16 [32768, 1024], P(('dp', 'tensor'))
- grad_tokens: bfloat16 [32768, 1024], P('dp')
- grad_gain_one: float32 [1024], replicated
- grad_gain_two: float32 [1024], replicated
- grad_w_query: float32 [1024, 1024], P(None, 'tensor')
- grad_w_key: float32 [512, 1024], P('tensor')
- grad_w_value: float32 [512, 1024], P('tensor')
- grad_w_out: float32 [1024, 1024], P('tensor')
- grad_w_gate: float32 [32, 512, 1024], P(None, 'tensor')
- grad_w_up: float32 [32, 512, 1024], P(None, 'tensor')
- grad_w_down: float32 [32, 512, 1024], P(None, 'tensor')
Inputs may be any that keep to these rules, and one draw needn't show every extreme that they name: `slot_index`: in each sequence group the 640 slots of one expert name distinct tokens of that group. `slot_gate`: in each expert's block the live slots (gate above zero) come first, followed by empty slots of gate zero; a block has 320 to 640 live slots, and in every sequence group some block is full.
All inputs are finite; a program needn't handle non-finite values.
Results may differ from a plain program's by a relative error of at most 0.023.
Values may be sent and summed in bfloat16 or wider, within the bound.
No kernel may reach another device: no remote copies, remote signals or barrier semaphores. Data moves between devices by JAX's collectives and lax.ppermute only.
A program may use at most 448 MiB of HBM per device.

v0:
```python
import math

import jax
import jax.numpy as jnp
from jax import lax
from jax.sharding import PartitionSpec as P

HD = 64
SEQ_LEN = 1024


EPS = 1e-05
THETA = 10000.0
MASKED = -1e30


def rope_tables(row_count, head_size):
    position = (jnp.arange(row_count) % SEQ_LEN).astype(jnp.float32)
    exponent = jnp.arange(head_size // 2).astype(jnp.float32) * (2.0 / head_size)
    angles = position[:, None] * jnp.power(THETA, -exponent)[None, :]
    return (jnp.cos(angles)[:, None, :], jnp.sin(angles)[:, None, :])


def rotate(values, cosine, sine_tab):
    half_size = values.shape[-1] // 2
    first, second = (values[..., :half_size], values[..., half_size:])
    return jnp.concatenate(
        [first * cosine - second * sine_tab, second * cosine + first * sine_tab], axis=-1
    )


def unrotate(grads_in, cosine, sine_tab):
    half_size = grads_in.shape[-1] // 2
    first, second = (grads_in[..., :half_size], grads_in[..., half_size:])
    return jnp.concatenate(
        [first * cosine + second * sine_tab, second * cosine - first * sine_tab], axis=-1
    )


def normalize(values, gain):
    inverse = lax.rsqrt(jnp.mean(values * values, axis=-1, keepdims=True) + EPS)
    return (values * inverse * gain, inverse)


def norm_back(values, inverse, gain, grad_normed):
    scaled = grad_normed * gain
    return inverse * scaled - values * inverse**3 * jnp.mean(
        scaled * values, axis=-1, keepdims=True
    )


def causal_mask(length):
    query_pos = lax.broadcasted_iota(jnp.int32, (length, length), 0)
    key_pos = lax.broadcasted_iota(jnp.int32, (length, length), 1)
    return key_pos <= query_pos


def attend_forward(members):
    queries, keys, values = members
    score_scale = queries.shape[-1] ** (-0.5)
    scores = (
        jnp.einsum("qgrd,kgd->grqk", queries, keys, preferred_element_type=jnp.float32)
        * score_scale
    )
    scores = jnp.where(causal_mask(queries.shape[0]), scores, MASKED)
    row_peak = jnp.max(scores, axis=-1, keepdims=True)
    exponent = jnp.exp(scores - row_peak)
    row_total = jnp.sum(exponent, axis=-1, keepdims=True)
    weights = (exponent / row_total).astype(jnp.bfloat16)
    mixed = jnp.einsum(
        "grqk,kgd->qgrd", weights, values, preferred_element_type=jnp.float32
    ).astype(jnp.bfloat16)
    return (mixed, row_peak[..., 0] + jnp.log(row_total[..., 0]))


def attend_backward(members):
    queries, keys, values, grad_mixed, log_total = members
    score_scale = queries.shape[-1] ** (-0.5)
    scores = (
        jnp.einsum("qgrd,kgd->grqk", queries, keys, preferred_element_type=jnp.float32)
        * score_scale
    )
    scores = jnp.where(causal_mask(queries.shape[0]), scores, MASKED)
    weights = jnp.exp(scores - log_total[..., None])
    grad_weights = jnp.einsum(
        "qgrd,kgd->grqk", grad_mixed, values, preferred_element_type=jnp.float32
    )
    grad_values = jnp.einsum(
        "grqk,qgrd->kgd",
        weights.astype(jnp.bfloat16),
        grad_mixed,
        preferred_element_type=jnp.float32,
    )
    row_delta = jnp.sum(grad_weights * weights, axis=-1, keepdims=True)
    grad_scores = (weights * (grad_weights - row_delta)).astype(jnp.bfloat16)
    grad_queries = (
        jnp.einsum("grqk,kgd->qgrd", grad_scores, keys, preferred_element_type=jnp.float32)
        * score_scale
    )
    grad_keys = (
        jnp.einsum("grqk,qgrd->kgd", grad_scores, queries, preferred_element_type=jnp.float32)
        * score_scale
    )
    return (grad_queries, grad_keys, grad_values)


def per_device(
    tokens,
    gain_one,
    gain_two,
    w_query,
    w_key,
    w_value,
    w_out,
    w_gate,
    w_up,
    w_down,
    slot_index,
    slot_gate,
    grad_output,
):
    n_tensor = lax.axis_size("tensor")
    shard_rows, width = tokens.shape
    head_size = HD
    local_heads = w_query.shape[1] // head_size
    local_groups = w_key.shape[0] // head_size
    expert_count, hidden_local, _ = w_gate.shape
    sweeps = math.gcd(expert_count, 4)
    slot_rows = slot_index[0].reshape(sweeps, expert_count // sweeps, -1)
    slot_weight = slot_gate[0].reshape(sweeps, expert_count // sweeps, -1)
    gate_blocks = w_gate.reshape(sweeps, expert_count // sweeps, hidden_local, width)
    up_blocks = w_up.reshape(sweeps, expert_count // sweeps, hidden_local, width)
    down_blocks = w_down.reshape(sweeps, expert_count // sweeps, hidden_local, width)
    row_start = lax.axis_index("tensor") * shard_rows
    full_rows = lax.all_gather(tokens, "tensor", axis=0, tiled=True)
    row_count = full_rows.shape[0]
    seq_count = row_count // SEQ_LEN
    cosine, sine_tab = rope_tables(row_count, head_size)
    rows_float = full_rows.astype(jnp.float32)
    normed_one, inverse_one = normalize(rows_float, gain_one)
    normed_one = normed_one.astype(jnp.bfloat16)
    query_pre = jnp.dot(normed_one, w_query, preferred_element_type=jnp.float32)
    key_pre = jnp.einsum("td,kd->tk", normed_one, w_key, preferred_element_type=jnp.float32)
    values = jnp.einsum(
        "td,kd->tk", normed_one, w_value, preferred_element_type=jnp.float32
    ).astype(jnp.bfloat16)
    queries = rotate(query_pre.reshape(row_count, local_heads, head_size), cosine, sine_tab).astype(
        jnp.bfloat16
    )
    keys = rotate(key_pre.reshape(row_count, local_groups, head_size), cosine, sine_tab).astype(
        jnp.bfloat16
    )
    seq_queries = queries.reshape(
        seq_count, SEQ_LEN, local_groups, local_heads // local_groups, head_size
    )
    seq_keys = keys.reshape(seq_count, SEQ_LEN, local_groups, head_size)
    seq_values = values.reshape(seq_count, SEQ_LEN, local_groups, head_size)
    mixed, log_total = lax.map(attend_forward, (seq_queries, seq_keys, seq_values))
    mixed = mixed.reshape(row_count, local_heads * head_size)
    attn_part = jnp.dot(mixed, w_out, preferred_element_type=jnp.float32)
    attn_shard = lax.psum_scatter(attn_part, "tensor", scatter_dimension=0, tiled=True)
    residual = tokens.astype(jnp.float32) + attn_shard
    normed_shard, inverse_two = normalize(residual, gain_two)
    normed_two = lax.all_gather(normed_shard.astype(jnp.bfloat16), "tensor", axis=0, tiled=True)

    def expert_forward(running, members):
        slot_part, weight_part, gate_part, up_part, down_part = members
        gathered = normed_two[slot_part]
        gate_pre = jnp.einsum(
            "ecd,efd->ecf", gathered, gate_part, preferred_element_type=jnp.float32
        )
        up_pre = jnp.einsum("ecd,efd->ecf", gathered, up_part, preferred_element_type=jnp.float32)
        active = (jax.nn.silu(gate_pre) * up_pre).astype(jnp.bfloat16)
        expert_out = (
            jnp.einsum("ecf,efd->ecd", active, down_part, preferred_element_type=jnp.float32)
            * weight_part[..., None]
        )
        running = running.at[slot_part.reshape(-1)].add(expert_out.reshape(-1, width))
        return (running, ())

    mixture_part, saved = lax.scan(
        expert_forward,
        jnp.zeros((row_count, width), jnp.float32),
        (slot_rows, slot_weight, gate_blocks, up_blocks, down_blocks),
    )
    mixture = lax.psum_scatter(
        mixture_part.astype(jnp.bfloat16), "tensor", scatter_dimension=0, tiled=True
    ).astype(jnp.float32)
    output = (residual + mixture).astype(jnp.bfloat16)
    grad_full = lax.all_gather(grad_output, "tensor", axis=0, tiled=True)

    def expert_backward(running, members):
        slot_part, weight_part, gate_part, up_part, down_part, kept_part = members
        gathered = normed_two[slot_part]
        gate_pre = jnp.einsum(
            "ecd,efd->ecf", gathered, gate_part, preferred_element_type=jnp.float32
        )
        up_pre = jnp.einsum("ecd,efd->ecf", gathered, up_part, preferred_element_type=jnp.float32)
        sigmoid_val = jax.nn.sigmoid(gate_pre)
        silu_val = gate_pre * sigmoid_val
        active = (silu_val * up_pre).astype(jnp.bfloat16)
        grad_out = (grad_full[slot_part].astype(jnp.float32) * weight_part[..., None]).astype(
            jnp.bfloat16
        )
        grad_act = jnp.einsum(
            "ecd,efd->ecf", grad_out, down_part, preferred_element_type=jnp.float32
        )
        grad_gate = (
            grad_act * up_pre * sigmoid_val * (1.0 + gate_pre * (1.0 - sigmoid_val))
        ).astype(jnp.bfloat16)
        grad_up = (grad_act * silu_val).astype(jnp.bfloat16)
        grad_down_w = jnp.einsum(
            "ecf,ecd->efd", active, grad_out, preferred_element_type=jnp.float32
        )
        grad_gate_w = jnp.einsum(
            "ecf,ecd->efd", grad_gate, gathered, preferred_element_type=jnp.float32
        )
        grad_up_w = jnp.einsum(
            "ecf,ecd->efd", grad_up, gathered, preferred_element_type=jnp.float32
        )
        grad_gathered = jnp.einsum(
            "ecf,efd->ecd", grad_gate, gate_part, preferred_element_type=jnp.float32
        )
        grad_gathered = grad_gathered + jnp.einsum(
            "ecf,efd->ecd", grad_up, up_part, preferred_element_type=jnp.float32
        )
        running = running.at[slot_part.reshape(-1)].add(grad_gathered.reshape(-1, width))
        grad_triple = (grad_gate_w, grad_up_w, grad_down_w)
        return (running, grad_triple)

    grad_normed_part, expert_grads = lax.scan(
        expert_backward,
        jnp.zeros((row_count, width), jnp.float32),
        (slot_rows, slot_weight, gate_blocks, up_blocks, down_blocks, saved),
    )
    grad_w_gate = expert_grads[0].reshape(expert_count, hidden_local, width)
    grad_w_up = expert_grads[1].reshape(expert_count, hidden_local, width)
    grad_w_down = expert_grads[2].reshape(expert_count, hidden_local, width)
    shared = (
        lax.psum_scatter(
            grad_w_gate.astype(jnp.bfloat16), "dp", scatter_dimension=2, tiled=True
        ).astype(jnp.float32),
        lax.psum_scatter(
            grad_w_up.astype(jnp.bfloat16), "dp", scatter_dimension=2, tiled=True
        ).astype(jnp.float32),
        lax.psum_scatter(
            grad_w_down.astype(jnp.bfloat16), "dp", scatter_dimension=2, tiled=True
        ).astype(jnp.float32),
    )
    grad_w_gate, grad_w_up, grad_w_down = (
        lax.all_gather(shared[0].astype(jnp.bfloat16), "dp", axis=2, tiled=True).astype(
            jnp.float32
        ),
        lax.all_gather(shared[1].astype(jnp.bfloat16), "dp", axis=2, tiled=True).astype(
            jnp.float32
        ),
        lax.all_gather(shared[2].astype(jnp.bfloat16), "dp", axis=2, tiled=True).astype(
            jnp.float32
        ),
    )
    grad_normed_two = lax.psum_scatter(
        grad_normed_part.astype(jnp.bfloat16), "tensor", scatter_dimension=0, tiled=True
    ).astype(jnp.float32)
    gain_two_part = jnp.sum(grad_normed_two * residual * inverse_two, axis=0)
    grad_resid = grad_output.astype(jnp.float32) + norm_back(
        residual, inverse_two, gain_two, grad_normed_two
    )
    grad_attn = lax.all_gather(grad_resid.astype(jnp.bfloat16), "tensor", axis=0, tiled=True)
    grad_w_out = jnp.dot(mixed.T, grad_attn, preferred_element_type=jnp.float32)
    grad_mixed = jnp.dot(grad_attn, w_out.T, preferred_element_type=jnp.float32).astype(
        jnp.bfloat16
    )
    grad_mixed = grad_mixed.reshape(
        seq_count, SEQ_LEN, local_groups, local_heads // local_groups, head_size
    )
    grad_q_rot, grad_k_rot, grad_v_seq = lax.map(
        attend_backward, (seq_queries, seq_keys, seq_values, grad_mixed, log_total)
    )
    grad_q = unrotate(grad_q_rot.reshape(row_count, local_heads, head_size), cosine, sine_tab)
    grad_q = grad_q.reshape(row_count, local_heads * head_size).astype(jnp.bfloat16)
    grad_k = unrotate(grad_k_rot.reshape(row_count, local_groups, head_size), cosine, sine_tab)
    grad_k = grad_k.reshape(row_count, local_groups * head_size).astype(jnp.bfloat16)
    grad_v = grad_v_seq.reshape(row_count, local_groups * head_size).astype(jnp.bfloat16)
    grad_w_query = jnp.dot(normed_one.T, grad_q, preferred_element_type=jnp.float32)
    grad_w_key = jnp.dot(grad_k.T, normed_one, preferred_element_type=jnp.float32)
    grad_w_value = jnp.dot(grad_v.T, normed_one, preferred_element_type=jnp.float32)
    grad_normed_one = jnp.dot(grad_q, w_query.T, preferred_element_type=jnp.float32)
    grad_normed_one = grad_normed_one + jnp.dot(grad_k, w_key, preferred_element_type=jnp.float32)
    grad_normed_one = grad_normed_one + jnp.dot(grad_v, w_value, preferred_element_type=jnp.float32)
    gain_one_part = jnp.sum(grad_normed_one * rows_float * inverse_one, axis=0)
    gains_tile = jnp.broadcast_to(
        jnp.stack([gain_one_part, gain_two_part])[None], (n_tensor, 2, width)
    )
    grad_normed_shard, gains_sum = (
        lax.psum_scatter(
            grad_normed_one.astype(jnp.bfloat16), "tensor", scatter_dimension=0, tiled=True
        ).astype(jnp.float32),
        lax.psum_scatter(
            gains_tile.astype(jnp.bfloat16), "tensor", scatter_dimension=0, tiled=True
        ).astype(jnp.float32),
    )
    inverse_shard = lax.dynamic_slice_in_dim(inverse_one, row_start, shard_rows, 0)
    grad_input = grad_resid + norm_back(
        tokens.astype(jnp.float32), inverse_shard, gain_one, grad_normed_shard
    )
    grad_tokens = lax.all_gather(grad_input.astype(jnp.bfloat16), "tensor", axis=0, tiled=True)
    grad_w_query, grad_w_key, grad_w_value, grad_w_out, gains_total = (
        lax.psum(grad_w_query.astype(jnp.bfloat16), "dp").astype(jnp.float32),
        lax.psum(grad_w_key.astype(jnp.bfloat16), "dp").astype(jnp.float32),
        lax.psum(grad_w_value.astype(jnp.bfloat16), "dp").astype(jnp.float32),
        lax.psum(grad_w_out.astype(jnp.bfloat16), "dp").astype(jnp.float32),
        lax.psum(gains_sum.astype(jnp.bfloat16), "dp").astype(jnp.float32),
    )
    return (
        output,
        grad_tokens,
        gains_total[0, 0],
        gains_total[0, 1],
        grad_w_query,
        grad_w_key,
        grad_w_value,
        grad_w_out,
        grad_w_gate,
        grad_w_up,
        grad_w_down,
    )


def solution(mesh):
    placed = (
        P(("dp", "tensor"), None),
        P(),
        P(),
        P(None, "tensor"),
        P("tensor", None),
        P("tensor", None),
        P("tensor", None),
        P(None, "tensor", None),
        P(None, "tensor", None),
        P(None, "tensor", None),
        P("dp", None, None),
        P("dp", None, None),
        P(("dp", "tensor"), None),
    )
    return jax.shard_map(
        per_device,
        mesh=mesh,
        in_specs=placed,
        out_specs=(
            P(("dp", "tensor"), None),
            P("dp", None),
            P(),
            P(),
            P(None, "tensor"),
            P("tensor", None),
            P("tensor", None),
            P("tensor", None),
            P(None, "tensor", None),
            P(None, "tensor", None),
            P(None, "tensor", None),
        ),
        check_vma=False,
    )
```

profile of v0, /device:TPU:0, one launch (start us, length us, event | category | flops | bytes accessed | tf_op | source)
XLA Modules:
  0.0 3397.9 jit_solution(16931180885736290006)
XLA Ops:
  9.8 59.3 %all-gather.9.cloned.1.call-done = bf16[2048,1024]{1,0:T(8,128)(2,1)} async-done(((bf16[1024,1024]{1,0:T(8,128)(2,1)}), bf16[2048,1024]{1,0:T(8,128)(2,1)}) %all-gather.9.cloned.1.call-update) | async-done | bytes 4194320 | tf_op jit(solution)/shard_map/all_gather | solution.py:135
  109.0 92.2 %while.52 = (s32[]{:T(128)}, bf16[2,1024,4,2,64]{1,4,3,2,0:T(8,128)(2,1)S(1)}, f32[2,4,2,1024]{3,2,1,0:T(2,128)S(1)}, bf16[2,1024,4,64]{1,3,2,0:T(8,128)(2,1)}, ...) while((s32[]{:T(128)}, bf16[2,1024,4,2,64]{1,4,3,2,0:T(8,128)(2,1)S(1)}, ...), condition=%wide.region_4.5_spmd, body=%wide.region_1.4_spmd.sunk | while | flops 2249711616 | bytes 108267600 | solution.py:158
  211.9 98.6 %reduce-scatter.8.cloned.1.call-done = f32[1024,1024]{1,0:T(8,128)} async-done(((f32[2048,1024]{1,0:T(8,128)}), f32[1024,1024]{1,0:T(8,128)}) %reduce-scatter.8.cloned.1.call-update) | async-done | bytes 4194320 | tf_op jit(solution)/shard_map/reduce_scatter | solution.py:161
  317.2 51.8 %all-gather.13.cloned.1.call-done = bf16[2048,1024]{1,0:T(8,128)(2,1)} async-done(((bf16[1024,1024]{1,0:T(8,128)(2,1)}), bf16[2048,1024]{1,0:T(8,128)(2,1)}) %all-gather.13.cloned.1.call-update) | async-done | bytes 4194320 | tf_op jit(solution)/shard_map/all_gather | solution.py:190
  368.9 58.8 %all-gather.11.cloned.1.call-done = bf16[2048,1024]{1,0:T(8,128)(2,1)} async-done(((bf16[1024,1024]{1,0:T(8,128)(2,1)}), bf16[2048,1024]{1,0:T(8,128)(2,1)}) %all-gather.11.cloned.1.call-update) | async-done | bytes 4194320 | tf_op jit(solution)/shard_map/all_gather | solution.py:164
  432.2 820.3 %while.54 = (s32[]{:T(128)}, f32[2048,1024]{1,0:T(8,128)}, bf16[4,8,256,1024]{3,2,1,0:T(8,128)(2,1)}, bf16[4,8,256,1024]{3,2,1,0:T(8,128)(2,1)}, bf16[4,8,256,10...) while((s32[]{:T(128)}, f32[2048,1024]{1,0:T(8,128)}, ...), condition=%wide.region_13.14_spmd, body=%wide.region_11.13_spmd.sunk | while | flops 21541720064 | bytes 387395840 | solution.py:231
  435.2 28.4 gather_fusion.2
  463.6 28.4 gather_fusion.1
  585.8 51.6 %scatter_fusion.1 = f32[2048,1024]{1,0:T(8,128)} fusion(f32[2048,1024]{1,0:T(8,128)} %get-tuple-element.630, s32[5120]{0:T(1024)S(1)} %bitcast.412, f32[5120,1024]{1,0:T(8,128)} %bitcast.389), kind=kCustom, calls=%fused_computation.4.clone.1 | custom fusion | flops 5242880 | bytes 62935040 | tf_op jit(solution)/shard_map/while/body/eval_jaxpr/scatter-add | solution.py:227
  640.2 28.4 gather_fusion.2
  668.7 28.4 gather_fusion.1
  790.7 51.6 %scatter_fusion.1 = f32[2048,1024]{1,0:T(8,128)} fusion(f32[2048,1024]{1,0:T(8,128)} %get-tuple-element.630, s32[5120]{0:T(1024)S(1)} %bitcast.412, f32[5120,1024]{1,0:T(8,128)} %bitcast.389), kind=kCustom, calls=%fused_computation.4.clone.1 | custom fusion | flops 5242880 | bytes 62935040 | tf_op jit(solution)/shard_map/while/body/eval_jaxpr/scatter-add | solution.py:227
  845.1 28.4 gather_fusion.2
  873.5 28.4 gather_fusion.1
  995.6 51.6 %scatter_fusion.1 = f32[2048,1024]{1,0:T(8,128)} fusion(f32[2048,1024]{1,0:T(8,128)} %get-tuple-element.630, s32[5120]{0:T(1024)S(1)} %bitcast.412, f32[5120,1024]{1,0:T(8,128)} %bitcast.389), kind=kCustom, calls=%fused_computation.4.clone.1 | custom fusion | flops 5242880 | bytes 62935040 | tf_op jit(solution)/shard_map/while/body/eval_jaxpr/scatter-add | solution.py:227
  1050.1 28.4 gather_fusion.2
  1078.5 28.4 gather_fusion.1
  1200.5 51.6 %scatter_fusion.1 = f32[2048,1024]{1,0:T(8,128)} fusion(f32[2048,1024]{1,0:T(8,128)} %get-tuple-element.630, s32[5120]{0:T(1024)S(1)} %bitcast.412, f32[5120,1024]{1,0:T(8,128)} %bitcast.389), kind=kCustom, calls=%fused_computation.4.clone.1 | custom fusion | flops 5242880 | bytes 62935040 | tf_op jit(solution)/shard_map/while/body/eval_jaxpr/scatter-add | solution.py:227
  1258.6 54.4 %reduce-scatter.12.cloned.1.call-done = bf16[1024,1024]{1,0:T(8,128)(2,1)} async-done(((bf16[2048,1024]{1,0:T(8,128)(2,1)}), bf16[1024,1024]{1,0:T(8,128)(2,1)}) %reduce-scatter.12.cloned.1.call-update) | async-done | bytes 2097168 | tf_op jit(solution)/shard_map/reduce_scatter | solution.py:261
  1322.2 56.8 %all-gather.15.cloned.1.call-done = bf16[2048,1024]{1,0:T(8,128)(2,1)} async-done(((bf16[1024,1024]{1,0:T(8,128)(2,1)}), bf16[2048,1024]{1,0:T(8,128)(2,1)}) %all-gather.15.cloned.1.call-update) | async-done | bytes 4194320 | tf_op jit(solution)/shard_map/all_gather | solution.py:268
  1397.8 333.4 %while.55 = (s32[]{:T(128)}, f32[2,1024,4,2,64]{1,0,4,3,2:T(2,128)}, f32[2,1024,4,64]{1,0,3,2:T(2,128)}, bf16[2,1024,4,64]{1,3,2,0:T(8,128)(2,1)}, bf16[2,1024,4...) while((s32[]{:T(128)}, ...), condition=%wide.region_18.19_spmd, body=%wide.region_16.18_spmd.sunk | while | flops 5496365056 | bytes 282823840 | solution.py:276
  1431.6 24.7 fusion.240
  1456.4 28.1 fusion.241
  1527.8 36.6 %dynamic_update_slice.49 = f32[2,1024,4,2,64]{1,0,4,3,2:T(2,128)} dynamic-update-slice(f32[2,1024,4,2,64]{1,0,4,3,2:T(2,128)} %get-tuple-element.667, f32[1,1024,4,2,64]{1,0,4,3,2:T(1,128)S(1)} %copy.117, s32[]{:T(128)S(6)} %copy.157, s32[]{:T(128)} %constant.123.clone.1..sunk, s32[]{:T(128)} %constant.123.clone.1..sunk, s32[]{:T(128)} %constant.123.clone.1..sunk, s32[]{:T(128)} %constant.123.clone.1..sunk) | dynamic-update-slice | bytes 4194308 | tf_op jit(solution)/shard_map/while/body/jit(dynamic_update_index_in_dim)/dynamic_update_slice | solution.py:276
  1598.1 24.7 fusion.240
  1622.8 28.1 fusion.241
  1694.2 36.6 %dynamic_update_slice.49 = f32[2,1024,4,2,64]{1,0,4,3,2:T(2,128)} dynamic-update-slice(f32[2,1024,4,2,64]{1,0,4,3,2:T(2,128)} %get-tuple-element.667, f32[1,1024,4,2,64]{1,0,4,3,2:T(1,128)S(1)} %copy.117, s32[]{:T(128)S(6)} %copy.157, s32[]{:T(128)} %constant.123.clone.1..sunk, s32[]{:T(128)} %constant.123.clone.1..sunk, s32[]{:T(128)} %constant.123.clone.1..sunk, s32[]{:T(128)} %constant.123.clone.1..sunk) | dynamic-update-slice | bytes 4194308 | tf_op jit(solution)/shard_map/while/body/jit(dynamic_update_index_in_dim)/dynamic_update_slice | solution.py:276
  1769.2 432.4 %while.53 = (s32[]{:T(128)}, f32[2048,1024]{1,0:T(8,128)}, s32[4,8,640]{2,1,0:T(8,128)}, bf16[2048,1024]{1,0:T(8,128)(2,1)}, bf16[4,8,256,1024]{3,2,1,0:T(8,128)...) while((s32[]{:T(128)}, f32[2048,1024]{1,0:T(8,128)}, ...), condition=%wide.region_9.10_spmd, body=%wide.region_7.9_spmd.sunk | while | flops 8071449600 | bytes 149247088 | solution.py:181
  1771.7 28.4 gather_fusion
  1826.0 51.6 %scatter_fusion = f32[2048,1024]{1,0:T(8,128)} fusion(f32[2048,1024]{1,0:T(8,128)} %get-tuple-element.698, s32[5120]{0:T(1024)S(1)} %bitcast.413, f32[5120,1024]{1,0:T(8,128)} %bitcast.390), kind=kCustom, calls=%fused_computation.3.clone.1 | custom fusion | flops 5242880 | bytes 62935040 | tf_op jit(solution)/shard_map/while/body/eval_jaxpr/scatter-add | solution.py:178
  1879.8 28.4 gather_fusion
  1933.9 51.6 %scatter_fusion = f32[2048,1024]{1,0:T(8,128)} fusion(f32[2048,1024]{1,0:T(8,128)} %get-tuple-element.698, s32[5120]{0:T(1024)S(1)} %bitcast.413, f32[5120,1024]{1,0:T(8,128)} %bitcast.390), kind=kCustom, calls=%fused_computation.3.clone.1 | custom fusion | flops 5242880 | bytes 62935040 | tf_op jit(solution)/shard_map/while/body/eval_jaxpr/scatter-add | solution.py:178
  1987.8 28.4 gather_fusion
  2041.9 51.6 %scatter_fusion = f32[2048,1024]{1,0:T(8,128)} fusion(f32[2048,1024]{1,0:T(8,128)} %get-tuple-element.698, s32[5120]{0:T(1024)S(1)} %bitcast.413, f32[5120,1024]{1,0:T(8,128)} %bitcast.390), kind=kCustom, calls=%fused_computation.3.clone.1 | custom fusion | flops 5242880 | bytes 62935040 | tf_op jit(solution)/shard_map/while/body/eval_jaxpr/scatter-add | solution.py:178
  2095.8 28.4 gather_fusion
  2150.0 51.6 %scatter_fusion = f32[2048,1024]{1,0:T(8,128)} fusion(f32[2048,1024]{1,0:T(8,128)} %get-tuple-element.698, s32[5120]{0:T(1024)S(1)} %bitcast.413, f32[5120,1024]{1,0:T(8,128)} %bitcast.390), kind=kCustom, calls=%fused_computation.3.clone.1 | custom fusion | flops 5242880 | bytes 62935040 | tf_op jit(solution)/shard_map/while/body/eval_jaxpr/scatter-add | solution.py:178
  2310.2 135.2 %reduce-scatter.20.cloned.1.call-done = bf16[32,256,64]{1,0,2:T(8,128)(2,1)} async-done(((bf16[32,256,1024]{1,0,2:T(8,128)(2,1)}), bf16[32,256,64]{1,0,2:T(8,128)(2,1)}) %reduce-scatter.20.cloned.1.call-update) | async-done | bytes 1048592 | tf_op jit(solution)/shard_map/reduce_scatter | solution.py:246
  2445.4 182.1 %reduce-scatter.16.cloned.1.call-done = bf16[32,256,64]{1,0,2:T(8,128)(2,1)} async-done(((bf16[32,256,1024]{1,0,2:T(8,128)(2,1)}), bf16[32,256,64]{1,0,2:T(8,128)(2,1)}) %reduce-scatter.16.cloned.1.call-update) | async-done | bytes 1048592 | tf_op jit(solution)/shard_map/reduce_scatter | solution.py:240
  2627.6 182.2 %reduce-scatter.18.cloned.1.call-done = bf16[32,256,64]{1,0,2:T(8,128)(2,1)} async-done(((bf16[32,256,1024]{1,0,2:T(8,128)(2,1)}), bf16[32,256,64]{1,0,2:T(8,128)(2,1)}) %reduce-scatter.18.cloned.1.call-update) | async-done | bytes 1048592 | tf_op jit(solution)/shard_map/reduce_scatter | solution.py:243
  2816.2 31.2 psum.35
  2848.0 69.6 %all-reduce.4.cloned.1.call-done = (bf16[1024,512]{1,0:T(8,128)(2,1)}, bf16[256,1024]{1,0:T(8,128)(2,1)}, bf16[256,1024]{1,0:T(8,128)(2,1)}, bf16[512,1024]{1,0:T(8,128)(2,1)}) async-done(((bf16[1024,512]{1,0:T(8,128)(2,1)}, bf16[256,1024]{1,0:T(8,128)(2,1)}, bf16[256,1024]{1,0:T(8,128)(2,1)}, bf16[512,1024]{1,0:T(8,128)(2,1)}), (bf16[1024,512]{1,0:T(8,128)(2,1)}, bf16[256,1024]{1,0:T(8,128)(2,1)}, ...) | async-done | bytes 3145744 | tf_op jit(solution)/shard_map/psum | solution.py:308
  2925.3 50.2 %all-gather.17.cloned.1.call-done = bf16[2048,1024]{1,0:T(8,128)(2,1)} async-done(((bf16[1024,1024]{1,0:T(8,128)(2,1)}), bf16[2048,1024]{1,0:T(8,128)(2,1)}) %all-gather.17.cloned.1.call-update) | async-done | bytes 4194320 | tf_op jit(solution)/shard_map/all_gather | solution.py:306
  2975.6 128.9 %all-gather.23.cloned.1.call-done = bf16[32,256,1024]{1,0,2:T(8,128)(2,1)} async-done(((bf16[32,256,64]{1,0,2:T(8,128)(2,1)}), bf16[32,256,1024]{1,0,2:T(8,128)(2,1)}) %all-gather.23.cloned.1.call-update) | async-done | bytes 16777232 | tf_op jit(solution)/shard_map/all_gather | solution.py:257
  3104.5 27.8 copy.79
  3132.3 99.4 %all-gather.19.cloned.1.call-done = bf16[32,256,1024]{1,0,2:T(8,128)(2,1)} async-done(((bf16[32,256,64]{1,0,2:T(8,128)(2,1)}), bf16[32,256,1024]{1,0,2:T(8,128)(2,1)}) %all-gather.19.cloned.1.call-update) | async-done | bytes 16777232 | tf_op jit(solution)/shard_map/all_gather | solution.py:251
  3231.6 27.8 copy.77
  3259.4 99.3 %all-gather.21.cloned.1.call-done = bf16[32,256,1024]{1,0,2:T(8,128)(2,1)} async-done(((bf16[32,256,64]{1,0,2:T(8,128)(2,1)}), bf16[32,256,1024]{1,0,2:T(8,128)(2,1)}) %all-gather.21.cloned.1.call-update) | async-done | bytes 16777232 | tf_op jit(solution)/shard_map/all_gather | solution.py:254
  3358.7 27.5 copy.78
  (383 shorter events, 1007.2 us)
Async XLA Ops:
  7.2 198.1 %copy-start = (bf16[512,1024]{1,0:T(8,128)(2,1)S(1)}, bf16[512,1024]{1,0:T(8,128)(2,1)}, u32[]{:S(2)}) copy-start(bf16[512,1024]{1,0:T(8,128)(2,1)} %param.27) | copy-start | bytes 3145732
  7.2 65.1 %copy-start.51 = (f32[1024]{0:T(1024)S(1)}, f32[1024]{0:T(1024)}, u32[]{:S(2)}) copy-start(f32[1024]{0:T(1024)} %param.22) | copy-start | bytes 12292
  7.2 61.9 %all-gather.9.cloned.1.call-start = ((), (), s32[]{:S(2)}) async-start(), calls=%async_computation.7 | async-start | bytes 6291456 | tf_op jit(solution)/shard_map/all_gather | solution.py:135
  7.9 302.6 %reduce-scatter.8.cloned.1.call-start = ((), (), s32[]{:S(2)}) async-start(), calls=%async_computation.8 | async-start | bytes 12582912 | tf_op jit(solution)/shard_map/reduce_scatter | solution.py:161
  9.8 88.0 %copy-start.13 = (f32[2048,32]{0,1:T(8,128)}, f32[2048,32]{0,1:T(8,128)S(1)}, u32[]{:S(2)}) copy-start(f32[2048,32]{0,1:T(8,128)S(1)} %get-tuple-element.362) | copy-start | bytes 786436
  211.1 99.4 %copy-start.10 = (bf16[1024,1024]{1,0:T(8,128)(2,1)S(1)}, bf16[1024,1024]{1,0:T(8,128)(2,1)}, u32[]{:S(2)}) copy-start(bf16[1024,1024]{1,0:T(8,128)(2,1)} %param.21) | copy-start | bytes 6291460
  211.1 157.8 %all-gather.13.cloned.1.call-start = ((), (), s32[]{:S(2)}) async-start(), calls=%async_computation.11 | async-start | bytes 6291456 | tf_op jit(solution)/shard_map/all_gather | solution.py:190
  211.9 103.5 %copy-start.44 = (f32[1024]{0:T(1024)S(1)}, f32[1024]{0:T(1024)}, u32[]{:S(2)}) copy-start(f32[1024]{0:T(1024)} %param.23) | copy-start | bytes 12292
  211.9 215.9 %all-gather.11.cloned.1.call-start = ((), (), s32[]{:S(2)}) async-start(), calls=%async_computation.9 | async-start | bytes 6291456 | tf_op jit(solution)/shard_map/all_gather | solution.py:164
  317.1 995.9 %reduce-scatter.12.cloned.1.call-start = ((), (), s32[]{:S(2)}) async-start(), calls=%async_computation.12 | async-start | bytes 6291456 | tf_op jit(solution)/shard_map/reduce_scatter | solution.py:261
  492.0 10.5 copy-start.2
  535.3 10.4 copy-start.4
  545.7 9.4 copy-start.3
  566.3 19.4 copy-start.30
  697.1 10.5 copy-start.2
  740.2 10.4 copy-start.4
  750.6 9.3 copy-start.3
  771.2 19.4 copy-start.30
  902.0 10.5 copy-start.2
  945.2 10.4 copy-start.4
  955.6 9.4 copy-start.3
  976.2 19.4 copy-start.30
  1107.0 10.5 copy-start.2
  1150.1 10.4 copy-start.4
  1160.4 9.3 copy-start.3
  1181.0 19.4 copy-start.30
  1258.5 54.5 %copy-start.39 = (f32[1024]{0:T(1024)S(1)}, f32[1024]{0:T(1024)}, u32[]{:S(2)}) copy-start(f32[1024]{0:T(1024)} %copy-done.38) | copy-start | bytes 12292
  1258.5 54.5 %copy-start.45 = (f32[1024]{0:T(1024)S(1)}, f32[1024]{0:T(1024)}, u32[]{:S(2)}) copy-start(f32[1024]{0:T(1024)} %param.23) | copy-start | bytes 12292
  1258.5 59.9 %copy-start.12 = (bf16[1024,1024]{1,0:T(8,128)(2,1)S(1)}, bf16[1024,1024]{1,0:T(8,128)(2,1)}, u32[]{:S(2)}) copy-start(bf16[1024,1024]{1,0:T(8,128)(2,1)} %param.33) | copy-start | bytes 6291460
  1258.6 59.9 %copy-start.47 = (f32[1024]{0:T(1024)S(1)}, f32[1024]{0:T(1024)}, u32[]{:S(2)}) copy-start(f32[1024]{0:T(1024)} %get-tuple-element.366) | copy-start | bytes 12292
  1258.6 120.4 %all-gather.15.cloned.1.call-start = ((), (), s32[]{:S(2)}) async-start(), calls=%async_computation.13 | async-start | bytes 6291456 | tf_op jit(solution)/shard_map/all_gather | solution.py:268
  1322.1 976.1 %reduce-scatter.14.cloned.1.call-start = ((), (), s32[]{:S(2)}) async-start(), calls=%async_computation.14 | async-start | bytes 6291456 | tf_op jit(solution)/shard_map/reduce_scatter | solution.py:295
  1387.1 10.6 copy-start.37
  1731.2 6.7 copy-start.14
  1764.8 537.2 %reduce-scatter.10.cloned.1.call-start = ((), (), s32[]{:S(2)}) async-start(), calls=%async_computation.10 | async-start | bytes 6291456 | tf_op jit(solution)/shard_map/reduce_scatter | solution.py:186
  2207.7 237.7 %reduce-scatter.20.cloned.1.call-start = ((), (), s32[]{:S(2)}) async-start(), calls=%async_computation.20 | async-start | bytes 17825792 | tf_op jit(solution)/shard_map/reduce_scatter | solution.py:246
  2231.8 395.7 %reduce-scatter.16.cloned.1.call-start = ((), (), s32[]{:S(2)}) async-start(), calls=%async_computation.16 | async-start | bytes 17825792 | tf_op jit(solution)/shard_map/reduce_scatter | solution.py:240
  2256.3 553.5 %reduce-scatter.18.cloned.1.call-start = ((), (), s32[]{:S(2)}) async-start(), calls=%async_computation.18 | async-start | bytes 17825792 | tf_op jit(solution)/shard_map/reduce_scatter | solution.py:243
  2280.9 7.7 copy-start.18
  2280.9 636.7 %all-reduce.4.cloned.1.call-start = ((), (), s32[]{:S(2)}) async-start(), calls=%async_computation.22 | async-start | bytes 6291456 | tf_op jit(solution)/shard_map/psum | solution.py:308
  2281.6 7.0 copy-start.22
  2298.1 677.4 %all-gather.17.cloned.1.call-start = ((), (), s32[]{:S(2)}) async-start(), calls=%async_computation.15 | async-start | bytes 6291456 | tf_op jit(solution)/shard_map/all_gather | solution.py:306
  2310.1 499.8 %copy-start.58 = (u32[32]{0:T(128)S(1)}, u32[32]{0:T(128)}, u32[]{:S(2)}) copy-start(u32[32]{0:T(128)} %constant.138) | copy-start | bytes 388
  2310.1 500.4 %copy-start.53 = (bf16[1024]{0:T(1024)(128)(2,1)S(1)}, bf16[1024]{0:T(1024)(128)(2,1)}, u32[]{:S(2)}) copy-start(bf16[1024]{0:T(1024)(128)(2,1)} %get-tuple-element.266) | copy-start | bytes 6148
  2310.1 500.4 %copy-start.54 = (bf16[1024]{0:T(1024)(128)(2,1)S(1)}, bf16[1024]{0:T(1024)(128)(2,1)}, u32[]{:S(2)}) copy-start(bf16[1024]{0:T(1024)(128)(2,1)} %get-tuple-element.350) | copy-start | bytes 6148
  2310.1 794.4 %all-gather.23.cloned.1.call-start = ((), (), s32[]{:S(2)}) async-start(), calls=%async_computation.21 | async-start | bytes 17825792 | tf_op jit(solution)/shard_map/all_gather | solution.py:257
  2445.4 786.2 %all-gather.19.cloned.1.call-start = ((), (), s32[]{:S(2)}) async-start(), calls=%async_computation.17 | async-start | bytes 17825792 | tf_op jit(solution)/shard_map/all_gather | solution.py:251
  2627.6 731.2 %all-gather.21.cloned.1.call-start = ((), (), s32[]{:S(2)}) async-start(), calls=%async_computation.19 | async-start | bytes 17825792 | tf_op jit(solution)/shard_map/all_gather | solution.py:254
  (40 other events, 131.8 us)
Sparse Core Ops, SparseCore 0:
  9.6 59.4 all-gather.8
  211.3 99.2 reduce-scatter.7
  312.2 56.7 all-gather.12
  371.0 56.7 all-gather.10
  1258.7 54.3 reduce-scatter.11
  1322.2 56.7 all-gather.14
  1764.9 54.2 reduce-scatter.13
  2207.8 54.7 reduce-scatter.9
  2266.7 178.6 reduce-scatter.19
  2449.9 177.5 reduce-scatter.15
  2632.2 177.5 reduce-scatter.17
  2814.7 102.8 all-reduce.3
  2919.7 55.7 all-gather.16
  2977.6 126.8 all-gather.22
  3106.5 125.0 all-gather.18
  3233.6 125.0 all-gather.20
where the time goes:
time: 3420 us; the launch traced here: 3400 us
  waiting for transfers between devices  1330 us (39%)
  matrix products  749 us (22%)
  local copies, waits for them, and re-layouts  697 us (20%)
  other arithmetic  570 us (17%)
  blocking collectives  36.2 us (1%)
    scatter-add x4, other arithmetic, expert_backward(): running.at[slot_part.reshape(-1)].add(grad_gathered.reshape(-1, width))  206 us
    scatter-add x4, other arithmetic, expert_forward(): running.at[slot_part.reshape(-1)].add(expert_out.reshape(-1, width))  206 us
    reduce_scatter x1, waiting for transfers between devices, per_device(): lax.psum_scatter(grad_w_up.astype(jnp.bfloat16), 'dp', scatter_dimension=...  182 us
    reduce_scatter x1, waiting for transfers between devices, per_device(): lax.psum_scatter(grad_w_gate.astype(jnp.bfloat16), 'dp', scatter_dimensio...  182 us
    reduce_scatter x1, waiting for transfers between devices, per_device(): lax.psum_scatter(grad_w_down.astype(jnp.bfloat16), 'dp', scatter_dimensio...  135 us
    all_gather x1, waiting for transfers between devices, per_device(): lax.all_gather(shared[2].astype(jnp.bfloat16), 'dp', axis=2, tiled=True)  129 us
    dynamic_update_slice x8, local copies, waits for them, and re-layouts, per_device(): lax.map(attend_backward, (seq_queries, seq_keys, seq_values, grad_mixed,...  117 us
    gather x4, local copies, waits for them, and re-layouts, expert_backward(): grad_full[slot_part].astype(jnp.float32) * weight_part[..., None]  114 us
  transfers between devices with their start and end apart: 16, of which 14 were waited for; matrix products, arithmetic and copies ran while one was open for 18% of the time, Pallas kernels for 0%

commit v1 on v0

--- a/solution.py
+++ b/solution.py
@@ -3,6 +3,8 @@
 import jax
 import jax.numpy as jnp
 from jax import lax
+from jax.experimental import pallas as pl
+from jax.experimental.pallas import tpu as pltpu
 from jax.sharding import PartitionSpec as P
 
 HD = 64
@@ -104,7 +106,7 @@
     return (grad_queries, grad_keys, grad_values)
 
 
-def per_device(
+def per_device_general(
     tokens,
     gain_one,
     gain_two,
@@ -326,6 +328,525 @@
     )
 
 
+BLOCK = 16
+CHUNKS = 4
+
+
+def nt_dot(left, right):
+    return lax.dot_general(
+        left, right, (((1,), (1,)), ((), ())), preferred_element_type=jnp.float32
+    )
+
+
+def nn_dot(left, right):
+    return lax.dot_general(
+        left, right, (((1,), (0,)), ((), ())), preferred_element_type=jnp.float32
+    )
+
+
+def tn_dot(left, right):
+    return lax.dot_general(
+        left, right, (((0,), (0,)), ((), ())), preferred_element_type=jnp.float32
+    )
+
+
+def expert_body(first, last, experts, cap, rows, width, hidden):
+    tiles = width // 128
+    shard = rows // 2
+    piece = shard // 2
+
+    def body(*refs):
+        index_ref, gate_ref, live_ref, place_ref = refs[:4]
+        normed_own, normed_other, grad_own, grad_other = refs[4:8]
+        gate_w, up_w, down_w = refs[8:11]
+        refs = refs[11:]
+        if not first:
+            mix_in, back_in = refs[:2]
+            refs = refs[2:]
+        grads_ref = refs[0]
+        if last:
+            mix_own, mix_other, back_own, back_other = refs[1:5]
+            refs = refs[5:]
+        else:
+            mix_out, back_out = refs[1:3]
+            refs = refs[3:]
+        (table_n, table_g, sum_m, sum_b, stage_n, stage_g, flat_n, flat_g, sems) = refs
+        step = pl.program_id(0)
+        place = place_ref[0]
+
+        @pl.when(step == 0)
+        def _():
+            if not first:
+                copy_m = pltpu.make_async_copy(mix_in, sum_m, sems.at[0])
+                copy_b = pltpu.make_async_copy(back_in, sum_b, sems.at[1])
+                copy_m.start()
+                copy_b.start()
+            else:
+                sum_m[...] = jnp.zeros_like(sum_m)
+                sum_b[...] = jnp.zeros_like(sum_b)
+            jobs = []
+            for part in range(2):
+                for half in range(2):
+                    jobs.append(
+                        (normed_own, normed_other)[part].at[pl.ds(half * piece, piece), :]
+                    )
+                    jobs.append((grad_own, grad_other)[part].at[pl.ds(half * piece, piece), :])
+            flats = (flat_n, flat_g)
+            tables = (table_n, table_g)
+
+            def fetch(number):
+                kind = number % 2
+                return pltpu.make_async_copy(
+                    jobs[number], flats[kind].at[pl.ds(0, piece), :], sems.at[2 + kind]
+                )
+
+            fetch(0).start()
+            fetch(1).start()
+            for number in range(8):
+                part, half, kind = number // 4, (number // 2) % 2, number % 2
+                fetch(number).wait()
+                side = place if part == 0 else 1 - place
+                base = (side * shard + half * piece) * tiles
+                for tile in range(tiles):
+                    tables[kind][pl.ds(base + tile, piece, stride=tiles), :] = flats[kind][
+                        0:piece, tile * 128 : (tile + 1) * 128
+                    ].astype(jnp.float32)
+                if number + 2 < 8:
+                    fetch(number + 2).start()
+            if not first:
+                copy_m.wait()
+                copy_b.wait()
+
+        blocks = (live_ref[step] + (BLOCK - 1)) // BLOCK
+        offset = step * cap
+
+        def gather(block, carry):
+            start = block * BLOCK
+            for lane in range(BLOCK):
+                row = pl.multiple_of(index_ref[offset + start + lane] * tiles, tiles)
+                weight = gate_ref[offset + start + lane]
+                spot = pl.ds(pl.multiple_of((start + lane) * tiles, tiles), tiles)
+                stage_n[spot, :] = table_n[pl.ds(row, tiles), :]
+                stage_g[spot, :] = table_g[pl.ds(row, tiles), :] * weight
+            return carry
+
+        lax.fori_loop(0, blocks, gather, 0)
+
+        def clear(block, carry):
+            spot = pl.ds(pl.multiple_of(block * BLOCK * tiles, BLOCK * tiles), BLOCK * tiles)
+            stage_n[spot, :] = jnp.zeros((BLOCK * tiles, 128), jnp.float32)
+            stage_g[spot, :] = jnp.zeros((BLOCK * tiles, 128), jnp.float32)
+            return carry
+
+        lax.fori_loop(blocks, cap // BLOCK, clear, 0)
+        for tile in range(tiles):
+            columns = slice(tile * 128, (tile + 1) * 128)
+            flat_n[:, columns] = stage_n[pl.ds(tile, cap, stride=tiles), :].astype(jnp.bfloat16)
+            flat_g[:, columns] = stage_g[pl.ds(tile, cap, stride=tiles), :].astype(jnp.bfloat16)
+        gathered = flat_n[...]
+        grad_out = flat_g[...]
+        gate_pre = nt_dot(gathered, gate_w[0])
+        up_pre = nt_dot(gathered, up_w[0])
+        grad_act = nt_dot(grad_out, down_w[0])
+        sigmoid_val = jax.nn.sigmoid(gate_pre)
+        silu_val = gate_pre * sigmoid_val
+        active = (silu_val * up_pre).astype(jnp.bfloat16)
+        grad_gate = (
+            grad_act * up_pre * sigmoid_val * (1.0 + gate_pre * (1.0 - sigmoid_val))
+        ).astype(jnp.bfloat16)
+        grad_up = (grad_act * silu_val).astype(jnp.bfloat16)
+        expert_out = nn_dot(active, down_w[0])
+        grad_rows = nn_dot(grad_gate, gate_w[0]) + nn_dot(grad_up, up_w[0])
+        for tile in range(tiles):
+            columns = slice(tile * 128, (tile + 1) * 128)
+            stage_n[pl.ds(tile, cap, stride=tiles), :] = expert_out[:, columns]
+            stage_g[pl.ds(tile, cap, stride=tiles), :] = grad_rows[:, columns]
+        middle = hidden // 2
+        for kind, (left, right) in enumerate(
+            ((grad_gate, gathered), (grad_up, gathered), (active, grad_out))
+        ):
+            weight_grad = tn_dot(left, right).astype(jnp.bfloat16)
+            spot = slice(kind * middle, (kind + 1) * middle)
+            grads_ref[0, spot, :] = weight_grad[0:middle]
+            grads_ref[1, spot, :] = weight_grad[middle:hidden]
+
+        def scatter(block, carry):
+            start = block * BLOCK
+            spots, new_m, new_b = [], [], []
+            for lane in range(BLOCK):
+                row = pl.multiple_of(index_ref[offset + start + lane] * tiles, tiles)
+                weight = gate_ref[offset + start + lane]
+                spot = pl.ds(pl.multiple_of((start + lane) * tiles, tiles), tiles)
+                spots.append(row)
+                new_m.append(sum_m[pl.ds(row, tiles), :] + stage_n[spot, :] * weight)
+                new_b.append(sum_b[pl.ds(row, tiles), :] + stage_g[spot, :])
+            for lane in range(BLOCK):
+                sum_m[pl.ds(spots[lane], tiles), :] = new_m[lane]
+                sum_b[pl.ds(spots[lane], tiles), :] = new_b[lane]
+            return carry
+
+        lax.fori_loop(0, blocks, scatter, 0)
+
+        @pl.when(step == experts - 1)
+        def _():
+            if not last:
+                copy_m = pltpu.make_async_copy(sum_m, mix_out, sems.at[0])
+                copy_b = pltpu.make_async_copy(sum_b, back_out, sems.at[1])
+                copy_m.start()
+                copy_b.start()
+                copy_m.wait()
+                copy_b.wait()
+            else:
+                sums = (sum_b, sum_m)
+                flats = (flat_g, flat_n)
+                targets = ((back_other, mix_other), (back_own, mix_own))
+
+                def put(number):
+                    part, half, kind = number // 4, (number // 2) % 2, number % 2
+                    return pltpu.make_async_copy(
+                        flats[kind].at[pl.ds(0, piece), :],
+                        targets[part][kind].at[pl.ds(half * piece, piece), :],
+                        sems.at[2 + kind],
+                    )
+
+                for number in range(8):
+                    part, half, kind = number // 4, (number // 2) % 2, number % 2
+                    if number >= 2:
+                        put(number - 2).wait()
+                    side = 1 - place if part == 0 else place
+                    base = (side * shard + half * piece) * tiles
+                    for tile in range(tiles):
+                        flats[kind][0:piece, tile * 128 : (tile + 1) * 128] = sums[kind][
+                            pl.ds(base + tile, piece, stride=tiles), :
+                        ].astype(jnp.bfloat16)
+                    put(number).start()
+                put(6).wait()
+                put(7).wait()
+
+    return body
+
+
+def expert_chunk(first, last, number, place, index, weights, live, tables, params, sums):
+    experts = index.shape[0]
+    cap = index.shape[1]
+    shard, width = tables[0].shape
+    rows = 2 * shard
+    hidden = params[0].shape[1]
+    tiles = width // 128
+    any_spec = pl.BlockSpec(memory_space=pl.ANY)
+
+    def weight_map(step, *_):
+        return (number * experts + step, 0, 0)
+
+    def grads_map(step, *_):
+        return (step, 0, 0)
+
+    weight_spec = pl.BlockSpec((1, hidden, width), weight_map)
+    in_specs = [any_spec] * 4 + [weight_spec] * 3
+    operands = list(tables) + list(params)
+    if not first:
+        in_specs = in_specs + [any_spec] * 2
+        operands = operands + list(sums)
+    unit_rows = 3 * hidden // 2
+    out_specs = [pl.BlockSpec((2, unit_rows, width), grads_map)]
+    out_shape = [jax.ShapeDtypeStruct((2 * experts, unit_rows, width), jnp.bfloat16)]
+    aliases = {}
+    if last:
+        out_specs = out_specs + [any_spec] * 4
+        out_shape = out_shape + [jax.ShapeDtypeStruct((shard, width), jnp.bfloat16)] * 4
+    else:
+        out_specs = out_specs + [any_spec] * 2
+        out_shape = out_shape + [jax.ShapeDtypeStruct((rows * tiles, 128), jnp.float32)] * 2
+    flops = 18 * experts * cap * hidden * width
+    return pl.pallas_call(
+        expert_body(first, last, experts, cap, rows, width, hidden),
+        grid_spec=pltpu.PrefetchScalarGridSpec(
+            num_scalar_prefetch=4,
+            grid=(experts,),
+            in_specs=in_specs,
+            out_specs=out_specs,
+            scratch_shapes=[
+                pltpu.VMEM((rows * tiles, 128), jnp.float32),
+                pltpu.VMEM((rows * tiles, 128), jnp.float32),
+                pltpu.VMEM((rows * tiles, 128), jnp.float32),
+                pltpu.VMEM((rows * tiles, 128), jnp.float32),
+                pltpu.VMEM((cap * tiles, 128), jnp.float32),
+                pltpu.VMEM((cap * tiles, 128), jnp.float32),
+                pltpu.VMEM((cap, width), jnp.bfloat16),
+                pltpu.VMEM((cap, width), jnp.bfloat16),
+                pltpu.SemaphoreType.DMA((4,)),
+            ],
+        ),
+        out_shape=out_shape,
+        input_output_aliases=aliases,
+        compiler_params=pltpu.CompilerParams(
+            dimension_semantics=("arbitrary",), vmem_limit_bytes=60 * 1024 * 1024
+        ),
+        cost_estimate=pl.CostEstimate(
+            flops=flops, transcendentals=0, bytes_accessed=12 * experts * hidden * width + 40 * rows * width
+        ),
+        name="experts",
+    )(index.reshape(-1), weights.reshape(-1), live, place, *operands)
+
+
+def add_bf16(left, right):
+    return (left.astype(jnp.float32) + right.astype(jnp.float32)).astype(jnp.bfloat16)
+
+
+def sum_over_dp(units):
+    devices = lax.axis_size("dp")
+    depth = devices // 4
+    me = lax.axis_index("dp")
+    core, row, level = me % 2, (me // 2) % 2, me // 4
+    over_core = [(i, i ^ 1) for i in range(devices)]
+    over_row = [(i, i ^ 2) for i in range(devices)]
+    up = [(i, i + 4) for i in range(devices - 4)]
+    down = [(i + 4, i) for i in range(devices - 4)]
+    send = lambda value, pairs: lax.ppermute(value, "dp", pairs)
+    take = lambda value, start, size: lax.dynamic_slice_in_dim(value, start, size, 0)
+    half = devices // 2
+    got = send(take(units, (1 - core) * half, half), over_core)
+    units = add_bf16(take(units, core * half, half), got)
+    got = send(take(units, (1 - row) * depth, depth), over_row)
+    units = add_bf16(take(units, row * depth, depth), got)
+    got_up = got_down = None
+    for step in range(1, depth):
+        part_up = take(units, jnp.minimum(depth + level - step, depth - 1), 1)
+        part_down = take(units, jnp.maximum(level + step - depth, 0), 1)
+        if step > 1:
+            part_up = add_bf16(part_up, got_up)
+            part_down = add_bf16(part_down, got_down)
+        got_up = send(part_up, up)
+        got_down = send(part_down, down)
+    mine = (
+        take(units, level, 1).astype(jnp.float32)
+        + got_up.astype(jnp.float32)
+        + got_down.astype(jnp.float32)
+    ).astype(jnp.bfloat16)
+    ups, downs = [mine], [mine]
+    for step in range(1, depth):
+        ups.append(send(ups[-1], up))
+        downs.append(send(downs[-1], down))
+    line = [mine] + [
+        jnp.where(level >= step, ups[step], downs[depth - step]) for step in range(1, depth)
+    ]
+    line = jnp.concatenate(line, axis=0)
+    plane = jnp.concatenate([line, send(line, over_row)], axis=0)
+    return plane, send(plane, over_core)
+
+
+def spread(number, chunks, spot, parts, earlier):
+    half, unit_rows, width = parts[0].shape
+    middle = unit_rows // 3
+    depth = half // 2
+    experts = half
+
+    def body(spot_ref, mine_ref, other_ref, *refs):
+        outs = refs[-3:]
+
+        @pl.when(pl.program_id(0) < half)
+        def _():
+            for kind in range(3):
+                outs[kind][0] = mine_ref[0, kind * middle : (kind + 1) * middle, :].astype(
+                    jnp.float32
+                )
+
+        @pl.when(pl.program_id(0) >= half)
+        def _():
+            for kind in range(3):
+                outs[kind][0] = other_ref[0, kind * middle : (kind + 1) * middle, :].astype(
+                    jnp.float32
+                )
+
+    def out_map(step, spot_ref):
+        core = jnp.where(step >= half, 1 - spot_ref[0], spot_ref[0])
+        inside = lax.rem(step, half)
+        row = jnp.where(inside >= depth, 1 - spot_ref[1], spot_ref[1])
+        level = lax.rem(spot_ref[2] + depth - lax.rem(inside, depth), depth)
+        unit = core * half + row * depth + level
+        return (number * experts + unit // 2, lax.rem(unit, 2), 0)
+
+    out_spec = pl.BlockSpec((1, middle, width), out_map)
+    in_specs = [
+        pl.BlockSpec((1, unit_rows, width), lambda step, _: (jnp.minimum(step, half - 1), 0, 0)),
+        pl.BlockSpec((1, unit_rows, width), lambda step, _: (jnp.maximum(step - half, 0), 0, 0)),
+    ]
+    operands = list(parts)
+    aliases = {}
+    if earlier is not None:
+        in_specs = in_specs + [pl.BlockSpec(memory_space=pl.ANY)] * 3
+        operands = operands + list(earlier)
+        aliases = {3: 0, 4: 1, 5: 2}
+    return pl.pallas_call(
+        body,
+        grid_spec=pltpu.PrefetchScalarGridSpec(
+            num_scalar_prefetch=1,
+            grid=(2 * half,),
+            in_specs=in_specs,
+            out_specs=[out_spec] * 3,
+        ),
+        out_shape=[jax.ShapeDtypeStruct((chunks * experts, 2 * middle, width), jnp.float32)] * 3,
+        input_output_aliases=aliases,
+        compiler_params=pltpu.CompilerParams(dimension_semantics=("arbitrary",)),
+        cost_estimate=pl.CostEstimate(
+            flops=0, transcendentals=0, bytes_accessed=12 * half * unit_rows * width
+        ),
+        name="spread",
+    )(spot, *operands)
+
+
+def per_device_pair(
+    tokens,
+    gain_one,
+    gain_two,
+    w_query,
+    w_key,
+    w_value,
+    w_out,
+    w_gate,
+    w_up,
+    w_down,
+    slot_index,
+    slot_gate,
+    grad_output,
+):
+    rows, width = tokens.shape
+    experts, hidden, _ = w_gate.shape
+    swap = lambda value: lax.ppermute(value, "tensor", [(0, 1), (1, 0)])
+    place = lax.axis_index("tensor").astype(jnp.int32)
+    cosine, sine_tab = rope_tables(rows, HD)
+    w_other = [swap(value) for value in (w_query, w_key, w_value)]
+    grad_other = swap(grad_output)
+    out_other = swap(w_out)
+    rows_float = tokens.astype(jnp.float32)
+    normed_one, inverse_one = normalize(rows_float, gain_one)
+    normed_one = normed_one.astype(jnp.bfloat16)
+
+    def heads_forward(query_w, key_w, value_w):
+        groups = key_w.shape[0] // HD
+        heads = query_w.shape[1] // HD
+        query_pre = jnp.dot(normed_one, query_w, preferred_element_type=jnp.float32)
+        key_pre = nt_dot(normed_one, key_w)
+        values = nt_dot(normed_one, value_w).astype(jnp.bfloat16).reshape(rows, groups, HD)
+        queries = rotate(query_pre.reshape(rows, heads, HD), cosine, sine_tab)
+        queries = queries.astype(jnp.bfloat16).reshape(rows, groups, heads // groups, HD)
+        keys = rotate(key_pre.reshape(rows, groups, HD), cosine, sine_tab).astype(jnp.bfloat16)
+        mixed, log_total = attend_forward((queries, keys, values))
+        return (queries, keys, values, mixed.reshape(rows, heads * HD), log_total)
+
+    own = heads_forward(w_query, w_key, w_value)
+    other = heads_forward(*w_other)
+    residual = (
+        rows_float
+        + jnp.dot(own[3], w_out, preferred_element_type=jnp.float32)
+        + jnp.dot(other[3], out_other, preferred_element_type=jnp.float32)
+    )
+    normed_two, inverse_two = normalize(residual, gain_two)
+    normed_two = normed_two.astype(jnp.bfloat16)
+    normed_other = swap(normed_two)
+
+    index = slot_index[0]
+    weights = slot_gate[0]
+    live = jnp.sum((weights > 0.0).astype(jnp.int32), axis=1)
+    chunks = math.gcd(experts, CHUNKS)
+    per_chunk = experts // chunks
+    sums = None
+    summed = []
+    for number in range(chunks):
+        part = slice(number * per_chunk, (number + 1) * per_chunk)
+        result = expert_chunk(
+            number == 0,
+            number == chunks - 1,
+            number,
+            place[None],
+            index[part],
+            weights[part],
+            live[part],
+            (normed_two, normed_other, grad_output, grad_other),
+            (w_gate, w_up, w_down),
+            sums,
+        )
+        summed.append(sum_over_dp(result[0]))
+        sums = result[1:]
+    me = lax.axis_index("dp").astype(jnp.int32)
+    spot = jnp.stack([me % 2, (me // 2) % 2, me // 4])
+    expert_grads = None
+    for number in range(chunks):
+        expert_grads = spread(number, chunks, spot, summed[number], expert_grads)
+    mix_own, mix_other, back_own, back_other = sums
+    grad_normed_two = back_own.astype(jnp.float32) + swap(back_other).astype(jnp.float32)
+    output = (
+        residual + mix_own.astype(jnp.float32) + swap(mix_other).astype(jnp.float32)
+    ).astype(jnp.bfloat16)
+    gain_two_part = jnp.sum(grad_normed_two * residual * inverse_two, axis=0)
+    grad_resid = grad_output.astype(jnp.float32) + norm_back(
+        residual, inverse_two, gain_two, grad_normed_two
+    )
+    grad_attn = grad_resid.astype(jnp.bfloat16)
+
+    def heads_backward(saved, query_w, key_w, value_w, out_w):
+        queries, keys, values, mixed, log_total = saved
+        groups = keys.shape[1]
+        heads = queries.shape[1] * queries.shape[2]
+        out_grad = tn_dot(mixed, grad_attn)
+        grad_mixed = nt_dot(grad_attn, out_w).astype(jnp.bfloat16)
+        grad_q, grad_k, grad_v = attend_backward(
+            (queries, keys, values, grad_mixed.reshape(queries.shape), log_total)
+        )
+        grad_q = unrotate(grad_q.reshape(rows, heads, HD), cosine, sine_tab)
+        grad_q = grad_q.reshape(rows, heads * HD).astype(jnp.bfloat16)
+        grad_k = unrotate(grad_k, cosine, sine_tab)
+        grad_k = grad_k.reshape(rows, groups * HD).astype(jnp.bfloat16)
+        grad_v = grad_v.reshape(rows, groups * HD).astype(jnp.bfloat16)
+        weight_grads = (
+            tn_dot(normed_one, grad_q),
+            tn_dot(grad_k, normed_one),
+            tn_dot(grad_v, normed_one),
+            out_grad,
+        )
+        back = nt_dot(grad_q, query_w) + nn_dot(grad_k, key_w) + nn_dot(grad_v, value_w)
+        return (weight_grads, back)
+
+    theirs, back_two = heads_backward(other, *w_other, out_other)
+    mine, back_one = heads_backward(own, w_query, w_key, w_value, w_out)
+    grad_normed_one = back_one + back_two
+    gain_one_part = jnp.sum(grad_normed_one * rows_float * inverse_one, axis=0)
+    grad_input = (
+        grad_resid + norm_back(rows_float, inverse_one, gain_one, grad_normed_one)
+    ).astype(jnp.bfloat16)
+    input_other = swap(grad_input)
+    grad_tokens = jnp.where(
+        place == 0,
+        jnp.concatenate([grad_input, input_other], axis=0),
+        jnp.concatenate([input_other, grad_input], axis=0),
+    )
+    weight_grads = [
+        lax.psum(
+            (left + swap(right.astype(jnp.bfloat16)).astype(jnp.float32)).astype(jnp.bfloat16),
+            "dp",
+        ).astype(jnp.float32)
+        for left, right in zip(mine, theirs)
+    ]
+    gains = lax.psum(jnp.stack([gain_one_part, gain_two_part]), ("dp", "tensor"))
+    return (
+        output,
+        grad_tokens,
+        gains[0],
+        gains[1],
+        *weight_grads,
+        *expert_grads,
+    )
+
+
+def per_device(*operands):
+    rows = operands[0].shape[0]
+    experts = operands[7].shape[0]
+    fits = 2 * experts == CHUNKS * lax.axis_size("dp") and lax.axis_size("dp") % 8 == 0
+    if lax.axis_size("tensor") == 2 and rows == SEQ_LEN and fits:
+        return per_device_pair(*operands)
+    return per_device_general(*operands)
+
+
 def solution(mesh):
     placed = (
         P(("dp", "tensor"), None),

time: 3420 us -> 2000 us (0.58)
  local copies, waits for them, and re-layouts: 697 us -> 63.8 us
  matrix products: 749 us -> 239 us
  waiting for transfers between devices: 1330 us -> 853 us
  Pallas kernels: 0 us -> 384 us
  other arithmetic: 570 us -> 201 us
  starting transfers between devices: 0.65 us -> 157 us
    ppermute x0 -> x77, waiting for transfers between devices: none -> 824 us  [the longest x64 651 us: sum_over_dp(): send = lambda value, pairs: lax.ppermute(value, 'dp', pairs)]
    reduce_scatter x7 -> x0, waiting for transfers between devices: 653 us -> none  [the longest x1 182 us: per_device(): lax.psum_scatter(grad_w_up.astype(jnp.bfloat16), 'dp', scatter_dimension=...]
    all_gather x8 -> x0, waiting for transfers between devices: 605 us -> none  [the longest x1 129 us: per_device(): lax.all_gather(shared[2].astype(jnp.bfloat16), 'dp', axis=2, tiled=True)]
    dot_general x54 -> x24, matrix products: 563 us -> 44.5 us  [the longest x8 16.8 us: tn_dot(): lax.dot_general(left, right, (((0,), (0,)), ((), ())), preferred_element_...]
    scatter-add x8 -> x0, other arithmetic: 413 us -> none  [the longest x4 206 us: expert_backward(): running.at[slot_part.reshape(-1)].add(grad_gathered.reshape(-1, width))]
    pallas_call x0 -> x8, Pallas kernels: none -> 384 us  [the longest x4 312 us: expert_chunk(): pl.pallas_call(expert_body(first, last, experts, cap, rows, width, hidden...]
    gather x12 -> x0, local copies, waits for them, and re-layouts: 341 us -> none  [the longest x4 114 us: expert_backward(): grad_full[slot_part].astype(jnp.float32) * weight_part[..., None]]
    ppermute x0 -> x77, starting transfers between devices: none -> 157 us  [the longest x64 137 us: sum_over_dp(): send = lambda value, pairs: lax.ppermute(value, 'dp', pairs)]
  transfers between devices with their start and end apart: 16 -> 78, of which waited for: 14 -> 45; matrix products, arithmetic and copies ran while one was open for 18% -> 25% of each run, Pallas kernels for 0% -> 3%
where the time goes in v1:
time: 2000 us; the launch traced here: 1980 us
  waiting for transfers between devices  853 us (43%)
  Pallas kernels  384 us (19%)
  matrix products  239 us (12%)
  other arithmetic  201 us (10%)
  starting transfers between devices  157 us (8%)
  blocking collectives  70 us (4%)
  local copies, waits for them, and re-layouts  63.8 us (3%)
    ppermute x64, waiting for transfers between devices, sum_over_dp(): send = lambda value, pairs: lax.ppermute(value, 'dp', pairs)  651 us
    pallas_call x4, Pallas kernels, expert_chunk(): pl.pallas_call(expert_body(first, last, experts, cap, rows, width, hidden...  312 us
    ppermute x13, waiting for transfers between devices, per_device_pair(): swap = lambda value: lax.ppermute(value, 'tensor', [(0, 1), (1, 0)])  173 us
    ppermute x64, starting transfers between devices, sum_over_dp(): send = lambda value, pairs: lax.ppermute(value, 'dp', pairs)  137 us
    pallas_call x4, Pallas kernels, spread(): pl.pallas_call(body, grid_spec=pltpu.PrefetchScalarGridSpec(num_scalar_pr...  72.2 us
    psum x1, blocking collectives, per_device_pair(): lax.psum(jnp.stack([gain_one_part, gain_two_part]), ('dp', 'tensor'))  70 us
    dot_general x2, matrix products, attend_backward(): jnp.einsum('qgrd,kgd->grqk', grad_mixed, values, preferred_element_type=j...  58.8 us
    convert_element_type x20, other arithmetic, add_bf16(): (left.astype(jnp.float32) + right.astype(jnp.float32)).astype(jnp.bfloat16)  56.7 us
  transfers between devices with their start and end apart: 78, of which 45 were waited for; matrix products, arithmetic and copies ran while one was open for 25% of the time, Pallas kernels for 3%

profile of v1, /device:TPU:0, one launch (start us, length us, event | category | flops | bytes accessed | tf_op | source)
XLA Modules:
  0.0 1983.7 jit_solution(4087786153676167244)
XLA Ops:
  35.3 21.7 %collective-permute-done.2 = bf16[1024,512]{1,0:T(8,128)(2,1)S(1)} collective-permute-done((bf16[1024,512]{1,0:T(8,128)(2,1)}, bf16[1024,512]{1,0:T(8,128)(2,1)S(1)}, u32[]{:S(2)}, u32[]{:S(2)}) %collective-permute-start.2) | collective-permute-done | bytes 1048608 | tf_op jit(solution)/shard_map/ppermute | solution.py:715
  59.1 14.5 fusion.51
  73.6 23.8 %fusion.19 = (f32[4,2,1024]{2,1,0:T(2,128)S(1)}, f32[4,2,1024]{2,1,0:T(2,128)S(1)}, f32[4,1024,1024,2]{2,1,3,0:T(8,128)}) fusion(pred[1024,1024]{0,1:T(8,128)(4,1)S(1)} %iota_compare_fusion, f32[4,1024,1024,2]{2,1,3,0:T(8,128)} %fusion.51, bf16[1024,4,2,32]{0,3,2,1:T(8,128)(2,1)S(1)} %bitcast.242, bf16[1024,4,2,32]{0,3,2,1:T(8,128)(2,1)S(1)} %bitcast.244, ...), kind=kOutput, calls=%fused_computation.33 | convolution fusion | flops 1127202816 | bytes 69795840 | tf_op jit(solution)/shard_map/qgrd,kgd->grqk/dot_general | solution.py:64
  97.5 23.7 %fusion.7 = (f32[4,2,1024]{2,1,0:T(2,128)S(1)}, f32[4,2,1024]{2,1,0:T(2,128)S(1)}) fusion(f32[4,2,1024]{2,1,0:T(2,128)S(1)} %get-tuple-element.71, f32[4,1024,1024,2]{2,1,3,0:T(8,128)} %get-tuple-element.175, pred[1024,1024]{0,1:T(8,128)(4,1)S(1)} %iota_compare_fusion, f32[4,2,1024]{2,1,0:T(2,128)S(1)} %get-tuple-element.72, f32[4,1024,1024,2]{2,1,3,0:T(8,128)} %fusion.51), kind=kLoop, calls=%fused_computation.19 | loop fusion | flops 67092480 | bytes 68288512 | tf_op jit(solution)/shard_map/reduce_sum | solution.py:70
  121.3 14.6 fusion.32
  135.9 15.1 fusion.33
  166.1 38.4 %collective-permute-done.4.refs_5_ = bf16[1024,1024]{1,0:T(8,128)(2,1)} collective-permute-done((bf16[1024,1024]{1,0:T(8,128)(2,1)S(1)}, bf16[1024,1024]{1,0:T(8,128)(2,1)}, u32[]{:S(2)}, u32[]{:S(2)}) %collective-permute-start.4) | collective-permute-done | bytes 2097184 | tf_op jit(solution)/shard_map/ppermute | solution.py:715
  204.5 73.9 %experts.4 = (bf16[16,384,1024]{2,1,0:T(8,128)(2,1)}, f32[16384,128]{1,0:T(8,128)}, f32[16384,128]{1,0:T(8,128)}) custom-call(s32[5120]{0:T(1024)} %reshape.257.refs_0_, f32[5120]{0:T(1024)} %reshape.258.refs_1_, s32[8]{0:T(128)} %get-tuple-element.171.refs_2_, s32[1]{0:T(128)} %bitcast.24.refs_3_, bf16[1024,1024]{1,0:T(8,128)(2,1)} %copy-done.37, ...), custom_call_target="tpu_custom_call" | custom-call | flops 24159191040 | bytes 109051904 | tf_op jit(solution)/shard_map/experts/pallas_call | solution.py:561
  278.5 81.1 %experts.5 = (bf16[16,384,1024]{2,1,0:T(8,128)(2,1)}, f32[16384,128]{1,0:T(8,128)}, f32[16384,128]{1,0:T(8,128)}) custom-call(s32[5120]{0:T(1024)} %reshape.255.refs_0_, f32[5120]{0:T(1024)} %reshape.256.refs_1_, s32[8]{0:T(128)} %get-tuple-element.172.refs_2_, s32[1]{0:T(128)} %bitcast.24.refs_3_, bf16[1024,1024]{1,0:T(8,128)(2,1)} %copy-done.37, ...), custom_call_target="tpu_custom_call" | custom-call | flops 24159191040 | bytes 109051904 | tf_op jit(solution)/shard_map/experts/pallas_call | solution.py:561
  359.6 76.1 %experts.6 = (bf16[16,384,1024]{2,1,0:T(8,128)(2,1)}, f32[16384,128]{1,0:T(8,128)}, f32[16384,128]{1,0:T(8,128)}) custom-call(s32[5120]{0:T(1024)} %reshape.253.refs_0_, f32[5120]{0:T(1024)} %reshape.254.refs_1_, s32[8]{0:T(128)} %get-tuple-element.173.refs_2_, s32[1]{0:T(128)} %bitcast.24.refs_3_, bf16[1024,1024]{1,0:T(8,128)(2,1)} %copy-done.37, ...), custom_call_target="tpu_custom_call" | custom-call | flops 24159191040 | bytes 109051904 | tf_op jit(solution)/shard_map/experts/pallas_call | solution.py:561
  435.7 80.6 %experts.7 = (bf16[16,384,1024]{2,1,0:T(8,128)(2,1)}, bf16[1024,1024]{1,0:T(8,128)(2,1)}, bf16[1024,1024]{1,0:T(8,128)(2,1)}, bf16[1024,1024]{1,0:T(8,128)(2,1)}, bf16[1024,1024]{1,0:T(8,128)(2,1)}) custom-call(s32[5120]{0:T(1024)} %reshape.251.refs_0_, f32[5120]{0:T(1024)} %reshape.252.refs_1_, s32[8]{0:T(128)} %get-tuple-element.174.refs_2_, ...), custom_call_target="tpu_custom_call" | custom-call | flops 24159191040 | bytes 109051904 | tf_op jit(solution)/shard_map/experts/pallas_call | solution.py:561
  541.5 23.6 %collective-permute-done.7 = bf16[1024,1024]{1,0:T(8,128)(2,1)S(1)} collective-permute-done((bf16[1024,1024]{1,0:T(8,128)(2,1)}, bf16[1024,1024]{1,0:T(8,128)(2,1)S(1)}, u32[]{:S(2)}, u32[]{:S(2)}) %collective-permute-start.7) | collective-permute-done | bytes 2097184 | tf_op jit(solution)/shard_map/ppermute | solution.py:715
  567.3 36.1 %collective-permute-done.6 = bf16[1024,1024]{1,0:T(8,128)(2,1)} collective-permute-done((bf16[1024,1024]{1,0:T(8,128)(2,1)}, bf16[1024,1024]{1,0:T(8,128)(2,1)}, u32[]{:S(2)}, u32[]{:S(2)}) %collective-permute-start.6) | collective-permute-done | bytes 2097184 | tf_op jit(solution)/shard_map/ppermute | solution.py:715
  612.7 14.1 fusion.83
  626.8 15.9 fusion.44
  642.6 44.8 %fusion.3 = (f32[4,2,1024]{2,1,0:T(2,128)S(1)}, f32[4,2,1024]{2,1,0:T(2,128)S(1)}, f32[4,1024,1024,2]{2,1,3,0:T(8,128)}) fusion(f32[4,2,1024]{2,1,0:T(2,128)S(1)} %bitcast.267, f32[4,1024,1024,2]{2,1,3,0:T(8,128)} %fusion.51, pred[1024,1024]{0,1:T(8,128)(4,1)S(1)} %iota_compare_fusion, f32[4,2,1024]{2,1,0:T(2,128)S(1)} %bitcast.265, ...), kind=kOutput, calls=%fused_computation.7 | convolution fusion | flops 1157611520 | bytes 136970240 | tf_op jit(solution)/shard_map/qgrd,kgd->grqk/dot_general | solution.py:87
  687.4 15.6 fusion.47
  703.0 55.5 %fusion.5 = (bf16[4,2,1024,1024]{2,3,1,0:T(8,128)(2,1)}, bf16[4,2,1024,1024]{2,3,1,0:T(8,128)(2,1)}) fusion(f32[4,1024,1024,2]{2,1,3,0:T(8,128)} %get-tuple-element.178, f32[4,2,1024]{2,1,0:T(2,128)S(1)} %get-tuple-element.67, f32[4,2,1024]{2,1,0:T(2,128)S(1)} %bitcast.269, f32[4,1024,1024,2]{2,1,3,0:T(8,128)} %fusion.51, ...), kind=kLoop, calls=%fused_computation.9 | loop fusion | flops 100663296 | bytes 168951808 | tf_op jit(solution)/shard_map/convert_element_type | solution.py:97
  810.0 12.3 fusion.35
  822.3 19.5 collective-permute-done.62
  850.2 59.1 %collective-permute-done.46 = bf16[4,384,1024]{2,1,0:T(8,128)(2,1)} collective-permute-done((bf16[4,384,1024]{2,1,0:T(8,128)(2,1)}, bf16[4,384,1024]{2,1,0:T(8,128)(2,1)}, u32[]{:S(2)}, u32[]{:S(2)}) %collective-permute-start.46) | collective-permute-done | bytes 3145760 | tf_op jit(solution)/shard_map/ppermute | solution.py:605
  916.0 60.7 %collective-permute-done.30 = bf16[4,384,1024]{2,1,0:T(8,128)(2,1)} collective-permute-done((bf16[4,384,1024]{2,1,0:T(8,128)(2,1)}, bf16[4,384,1024]{2,1,0:T(8,128)(2,1)}, u32[]{:S(2)}, u32[]{:S(2)}) %collective-permute-start.30) | collective-permute-done | bytes 3145760 | tf_op jit(solution)/shard_map/ppermute | solution.py:605
  991.6 48.7 %collective-permute-done.14 = bf16[4,384,1024]{2,1,0:T(8,128)(2,1)S(1)} collective-permute-done((bf16[4,384,1024]{2,1,0:T(8,128)(2,1)}, bf16[4,384,1024]{2,1,0:T(8,128)(2,1)S(1)}, u32[]{:S(2)}, u32[]{:S(2)}) %collective-permute-start.14) | collective-permute-done | bytes 3145760 | tf_op jit(solution)/shard_map/ppermute | solution.py:605
  1064.6 13.5 collective-permute-done.15
  1112.3 15.2 collective-permute-done.51
  1167.0 11.1 collective-permute-done.52
  1181.2 13.8 collective-permute-done.19
  1196.3 12.3 fusion.37
  1230.0 15.6 collective-permute-done.54
  1266.2 13.0 collective-permute-done.38
  1282.0 14.0 collective-permute-done.71
  1297.7 15.2 collective-permute-done.55
  1331.8 14.8 collective-permute-done.72
  1349.7 13.7 collective-permute-done.56
  1366.0 14.3 collective-permute-done.22
  1418.3 15.6 collective-permute-done.74
  1495.7 26.0 %collective-permute-done.75 = bf16[4,384,1024]{2,1,0:T(8,128)(2,1)S(1)} collective-permute-done((bf16[4,384,1024]{2,1,0:T(8,128)(2,1)S(1)}, bf16[4,384,1024]{2,1,0:T(8,128)(2,1)S(1)}, u32[]{:S(2)}, u32[]{:S(2)}) %collective-permute-start.75) | collective-permute-done | bytes 3145760 | tf_op jit(solution)/shard_map/ppermute | solution.py:605
  1523.8 65.5 %collective-permute-done.59 = bf16[4,384,1024]{2,1,0:T(8,128)(2,1)} collective-permute-done((bf16[4,384,1024]{2,1,0:T(8,128)(2,1)}, bf16[4,384,1024]{2,1,0:T(8,128)(2,1)}, u32[]{:S(2)}, u32[]{:S(2)}) %collective-permute-start.59) | collective-permute-done | bytes 3145760 | tf_op jit(solution)/shard_map/ppermute | solution.py:605
  1593.2 63.5 %collective-permute-done.43 = bf16[4,384,1024]{2,1,0:T(8,128)(2,1)} collective-permute-done((bf16[4,384,1024]{2,1,0:T(8,128)(2,1)}, bf16[4,384,1024]{2,1,0:T(8,128)(2,1)}, u32[]{:S(2)}, u32[]{:S(2)}) %collective-permute-start.43) | collective-permute-done | bytes 3145760 | tf_op jit(solution)/shard_map/ppermute | solution.py:605
  1660.7 51.3 %collective-permute-done.27 = bf16[4,384,1024]{2,1,0:T(8,128)(2,1)} collective-permute-done((bf16[4,384,1024]{2,1,0:T(8,128)(2,1)}, bf16[4,384,1024]{2,1,0:T(8,128)(2,1)}, u32[]{:S(2)}, u32[]{:S(2)}) %collective-permute-start.27) | collective-permute-done | bytes 3145760 | tf_op jit(solution)/shard_map/ppermute | solution.py:605
  1741.7 18.1 collective-permute-done.12
  1766.5 16.9 collective-permute-done.9
  1793.1 70.0 %psum.35 = f32[2,1024]{1,0:T(2,128)S(1)} all-reduce(f32[2,1024]{1,0:T(2,128)S(1)} %pad_maximum_fusion.14), channel_id=1, replica_groups=mesh['dp'=16,'tensor'=2] {'dp','tensor'}, use_global_device_ids=true, to_apply=%region_13.14 | all-reduce | flops 2048 | bytes 16384 | tf_op jit(solution)/shard_map/psum | solution.py:830
  1868.3 28.4 %all-reduce.3.cloned.1.call-done = (bf16[1024,512]{1,0:T(8,128)(2,1)}, bf16[256,1024]{1,0:T(8,128)(2,1)}, bf16[256,1024]{1,0:T(8,128)(2,1)}, bf16[512,1024]{1,0:T(8,128)(2,1)}) async-done(((bf16[1024,512]{1,0:T(8,128)(2,1)}, bf16[256,1024]{1,0:T(8,128)(2,1)}, bf16[256,1024]{1,0:T(8,128)(2,1)}, bf16[512,1024]{1,0:T(8,128)(2,1)}), (bf16[1024,512]{1,0:T(8,128)(2,1)}, bf16[256,1024]{1,0:T(8,128)(2,1)}, ...) | async-done | bytes 3145744 | tf_op jit(solution)/shard_map/psum | solution.py:824
  1904.5 18.1 spread.4
  1922.5 18.1 spread.5
  1940.6 18.1 spread.6
  1958.6 18.1 spread.7
  (443 shorter events, 503.9 us)
Async XLA Ops:
  7.2 1889.5 %all-reduce.3.cloned.1.call-start = ((), (), s32[]{:S(2)}) async-start(), calls=%async_computation | async-start | bytes 6291456 | tf_op jit(solution)/shard_map/psum | solution.py:824
  12.3 140.1 %collective-permute-start.3 = (bf16[512,1024]{1,0:T(8,128)(2,1)}, bf16[512,1024]{1,0:T(8,128)(2,1)}, u32[]{:S(2)}, u32[]{:S(2)}) collective-permute-start(bf16[512,1024]{1,0:T(8,128)(2,1)} %param.19), channel_id=1, source_target_pairs={{0,1},{1,0},{2,3},{3,2},{4,5},{5,4},{6,7},{7,6},{8,9},{9,8},{10,11... | collective-permute-start | bytes 3145736 | tf_op jit(solution)/shard_map/ppermute | solution.py:715
  12.3 153.8 %collective-permute-start.5 = (bf16[1024,1024]{1,0:T(8,128)(2,1)}, bf16[1024,1024]{1,0:T(8,128)(2,1)}, u32[]{:S(2)}, u32[]{:S(2)}) collective-permute-start(bf16[1024,1024]{1,0:T(8,128)(2,1)} %refs_6_.7), channel_id=1, source_target_pairs={{0,1},{1,0},{2,3},{3,2},{4,5},{5,4},{6,7},{7,6},{8,9},{9,8},{10,11... | collective-permute-start | bytes 6291464 | tf_op jit(solution)/shard_map/ppermute | solution.py:715
  517.8 85.6 %collective-permute-start.6 = (bf16[1024,1024]{1,0:T(8,128)(2,1)}, bf16[1024,1024]{1,0:T(8,128)(2,1)}, u32[]{:S(2)}, u32[]{:S(2)}) collective-permute-start(bf16[1024,1024]{1,0:T(8,128)(2,1)} %get-tuple-element.44), channel_id=1, source_target_pairs={{0,1},{1,0},{2,3},{3,2},{4,5},{5,4},{6,7},{7,6},{8,9},{9,8},{10,11... | collective-permute-start | bytes 6291464 | tf_op jit(solution)/shard_map/ppermute | solution.py:715
  524.9 233.7 %collective-permute-start.61 = (bf16[8,384,1024]{2,1,0:T(8,128)(2,1)}, bf16[8,384,1024]{2,1,0:T(8,128)(2,1)}, u32[]{:S(2)}, u32[]{:S(2)}) collective-permute-start(bf16[8,384,1024]{2,1,0:T(8,128)(2,1)} %constant_dynamic-slice_fusion.3), channel_id=1, source_target_pairs={{0,2},{2,0},{4,6},{6,4},{8,10},{10,8},{12,14},{14,12},{16,18},{18,... | collective-permute-start | bytes 18874376 | tf_op jit(solution)/shard_map/ppermute | solution.py:605
  531.2 241.3 %collective-permute-start.45 = (bf16[8,384,1024]{2,1,0:T(8,128)(2,1)}, bf16[8,384,1024]{2,1,0:T(8,128)(2,1)}, u32[]{:S(2)}, u32[]{:S(2)}) collective-permute-start(bf16[8,384,1024]{2,1,0:T(8,128)(2,1)} %constant_dynamic-slice_fusion.7), channel_id=1, source_target_pairs={{0,2},{2,0},{4,6},{6,4},{8,10},{10,8},{12,14},{14,12},{16,18},{18,... | collective-permute-start | bytes 18874376 | tf_op jit(solution)/shard_map/ppermute | solution.py:605
  535.2 249.1 %collective-permute-start.29 = (bf16[8,384,1024]{2,1,0:T(8,128)(2,1)}, bf16[8,384,1024]{2,1,0:T(8,128)(2,1)}, u32[]{:S(2)}, u32[]{:S(2)}) collective-permute-start(bf16[8,384,1024]{2,1,0:T(8,128)(2,1)} %constant_dynamic-slice_fusion.11), channel_id=1, source_target_pairs={{0,2},{2,0},{4,6},{6,4},{8,10},{10,8},{12,14},{14,12},{16,18},{18,... | collective-permute-start | bytes 18874376 | tf_op jit(solution)/shard_map/ppermute | solution.py:605
  565.1 230.7 %collective-permute-start.13 = (bf16[8,384,1024]{2,1,0:T(8,128)(2,1)}, bf16[8,384,1024]{2,1,0:T(8,128)(2,1)}, u32[]{:S(2)}, u32[]{:S(2)}) collective-permute-start(bf16[8,384,1024]{2,1,0:T(8,128)(2,1)} %constant_dynamic-slice_fusion.15), channel_id=1, source_target_pairs={{0,2},{2,0},{4,6},{6,4},{8,10},{10,8},{12,14},{14,12},{16,18},{18,... | collective-permute-start | bytes 18874376 | tf_op jit(solution)/shard_map/ppermute | solution.py:605
  768.7 73.1 %collective-permute-start.62 = (bf16[4,384,1024]{2,1,0:T(8,128)(2,1)}, bf16[4,384,1024]{2,1,0:T(8,128)(2,1)}, u32[]{:S(2)}, u32[]{:S(2)}) collective-permute-start(bf16[4,384,1024]{2,1,0:T(8,128)(2,1)} %constant_dynamic-slice_fusion.2), channel_id=1, source_target_pairs={{0,4},{2,6},{4,0},{6,2},{8,12},{10,14},{12,8},{14,10},{16,20},{18,... | collective-permute-start | bytes 9437192 | tf_op jit(solution)/shard_map/ppermute | solution.py:605
  782.9 126.4 %collective-permute-start.46 = (bf16[4,384,1024]{2,1,0:T(8,128)(2,1)}, bf16[4,384,1024]{2,1,0:T(8,128)(2,1)}, u32[]{:S(2)}, u32[]{:S(2)}) collective-permute-start(bf16[4,384,1024]{2,1,0:T(8,128)(2,1)} %constant_dynamic-slice_fusion.6), channel_id=1, source_target_pairs={{0,4},{2,6},{4,0},{6,2},{8,12},{10,14},{12,8},{14,10},{16,20},{18,... | collective-permute-start | bytes 9437192 | tf_op jit(solution)/shard_map/ppermute | solution.py:605
  794.4 182.2 %collective-permute-start.30 = (bf16[4,384,1024]{2,1,0:T(8,128)(2,1)}, bf16[4,384,1024]{2,1,0:T(8,128)(2,1)}, u32[]{:S(2)}, u32[]{:S(2)}) collective-permute-start(bf16[4,384,1024]{2,1,0:T(8,128)(2,1)} %constant_dynamic-slice_fusion.10), channel_id=1, source_target_pairs={{0,4},{2,6},{4,0},{6,2},{8,12},{10,14},{12,8},{14,10},{16,20},{18,... | collective-permute-start | bytes 9437192 | tf_op jit(solution)/shard_map/ppermute | solution.py:605
  808.7 231.6 %collective-permute-start.14 = (bf16[4,384,1024]{2,1,0:T(8,128)(2,1)}, bf16[4,384,1024]{2,1,0:T(8,128)(2,1)S(1)}, u32[]{:S(2)}, u32[]{:S(2)}) collective-permute-start(bf16[4,384,1024]{2,1,0:T(8,128)(2,1)} %constant_dynamic-slice_fusion.14), channel_id=1, source_target_pairs={{0,4},{2,6},{4,0},{6,2},{8,12},{10,14},{12,8},{14,10},{16,20},{18,... | collective-permute-start | bytes 9437192 | tf_op jit(solution)/shard_map/ppermute | solution.py:605
  847.2 135.0 %collective-permute-start.63 = (bf16[1,384,1024]{2,1,0:T(8,128)(2,1)S(1)}, bf16[1,384,1024]{2,1,0:T(8,128)(2,1)S(1)}, u32[]{:S(2)}, u32[]{:S(2)}) collective-permute-start(bf16[1,384,1024]{2,1,0:T(8,128)(2,1)S(1)} %get-tuple-element.115), channel_id=1, source_target_pairs={{0,8},{2,10},{4,12},{6,14},{8,16},{10,18},{12,20},{14,22},{16,24},... | collective-permute-start | bytes 2359304 | tf_op jit(solution)/shard_map/ppermute | solution.py:605
  848.6 206.0 %collective-permute-start.66 = (bf16[1,384,1024]{2,1,0:T(8,128)(2,1)}, bf16[1,384,1024]{2,1,0:T(8,128)(2,1)S(1)}, u32[]{:S(2)}, u32[]{:S(2)}) collective-permute-start(bf16[1,384,1024]{2,1,0:T(8,128)(2,1)} %get-tuple-element.116), channel_id=1, source_target_pairs={{8,0},{10,2},{12,4},{14,6},{16,8},{18,10},{20,12},{22,14},{24,16},... | collective-permute-start | bytes 2359304 | tf_op jit(solution)/shard_map/ppermute | solution.py:605
  914.6 72.5 %collective-permute-start.47 = (bf16[1,384,1024]{2,1,0:T(8,128)(2,1)S(1)}, bf16[1,384,1024]{2,1,0:T(8,128)(2,1)S(1)}, u32[]{:S(2)}, u32[]{:S(2)}) collective-permute-start(bf16[1,384,1024]{2,1,0:T(8,128)(2,1)S(1)} %get-tuple-element.119), channel_id=1, source_target_pairs={{0,8},{2,10},{4,12},{6,14},{8,16},{10,18},{12,20},{14,22},{16,24},... | collective-permute-start | bytes 2359304 | tf_op jit(solution)/shard_map/ppermute | solution.py:605
  976.7 84.6 %collective-permute-start.50 = (bf16[1,384,1024]{2,1,0:T(8,128)(2,1)}, bf16[1,384,1024]{2,1,0:T(8,128)(2,1)S(1)}, u32[]{:S(2)}, u32[]{:S(2)}) collective-permute-start(bf16[1,384,1024]{2,1,0:T(8,128)(2,1)} %get-tuple-element.120), channel_id=1, source_target_pairs={{8,0},{10,2},{12,4},{14,6},{16,8},{18,10},{20,12},{22,14},{24,16},... | collective-permute-start | bytes 2359304 | tf_op jit(solution)/shard_map/ppermute | solution.py:605
  982.2 64.7 %collective-permute-start.31 = (bf16[1,384,1024]{2,1,0:T(8,128)(2,1)S(1)}, bf16[1,384,1024]{2,1,0:T(8,128)(2,1)S(1)}, u32[]{:S(2)}, u32[]{:S(2)}) collective-permute-start(bf16[1,384,1024]{2,1,0:T(8,128)(2,1)S(1)} %get-tuple-element.123), channel_id=1, source_target_pairs={{0,8},{2,10},{4,12},{6,14},{8,16},{10,18},{12,20},{14,22},{16,24},... | collective-permute-start | bytes 2359304 | tf_op jit(solution)/shard_map/ppermute | solution.py:605
  987.2 68.7 %collective-permute-start.64 = (bf16[1,384,1024]{2,1,0:T(8,128)(2,1)S(1)}, bf16[1,384,1024]{2,1,0:T(8,128)(2,1)S(1)}, u32[]{:S(2)}, u32[]{:S(2)}) collective-permute-start(bf16[1,384,1024]{2,1,0:T(8,128)(2,1)S(1)} %add_convert_fusion.15), channel_id=1, source_target_pairs={{0,8},{2,10},{4,12},{6,14},{8,16},{10,18},{12,20},{14,22},{16,24},... | collective-permute-start | bytes 2359304 | tf_op jit(solution)/shard_map/ppermute | solution.py:605
  1061.2 67.9 %collective-permute-start.18 = (bf16[1,384,1024]{2,1,0:T(8,128)(2,1)S(1)}, bf16[1,384,1024]{2,1,0:T(8,128)(2,1)S(1)}, u32[]{:S(2)}, u32[]{:S(2)}) collective-permute-start(bf16[1,384,1024]{2,1,0:T(8,128)(2,1)S(1)} %get-tuple-element.128), channel_id=1, source_target_pairs={{8,0},{10,2},{12,4},{14,6},{16,8},{18,10},{20,12},{22,14},{24,16},... | collective-permute-start | bytes 2359304 | tf_op jit(solution)/shard_map/ppermute | solution.py:605
  1079.7 54.0 %collective-permute-start.16 = (bf16[1,384,1024]{2,1,0:T(8,128)(2,1)S(1)}, bf16[1,384,1024]{2,1,0:T(8,128)(2,1)S(1)}, u32[]{:S(2)}, u32[]{:S(2)}) collective-permute-start(bf16[1,384,1024]{2,1,0:T(8,128)(2,1)S(1)} %add_convert_fusion.30), channel_id=1, source_target_pairs={{0,8},{2,10},{4,12},{6,14},{8,16},{10,18},{12,20},{14,22},{16,24},... | collective-permute-start | bytes 2359304 | tf_op jit(solution)/shard_map/ppermute | solution.py:605
  1095.0 51.9 %collective-permute-start.65 = (bf16[1,384,1024]{2,1,0:T(8,128)(2,1)S(1)}, bf16[1,384,1024]{2,1,0:T(8,128)(2,1)S(1)}, u32[]{:S(2)}, u32[]{:S(2)}) collective-permute-start(bf16[1,384,1024]{2,1,0:T(8,128)(2,1)S(1)} %get-tuple-element.113), channel_id=1, source_target_pairs={{0,8},{2,10},{4,12},{6,14},{8,16},{10,18},{12,20},{14,22},{16,24},... | collective-permute-start | bytes 2359304 | tf_op jit(solution)/shard_map/ppermute | solution.py:605
  1144.4 50.7 %collective-permute-start.19 = (bf16[1,384,1024]{2,1,0:T(8,128)(2,1)S(1)}, bf16[1,384,1024]{2,1,0:T(8,128)(2,1)}, u32[]{:S(2)}, u32[]{:S(2)}) collective-permute-start(bf16[1,384,1024]{2,1,0:T(8,128)(2,1)S(1)} %get-tuple-element.126), channel_id=1, source_target_pairs={{8,0},{10,2},{12,4},{14,6},{16,8},{18,10},{20,12},{22,14},{24,16},... | collective-permute-start | bytes 2359304 | tf_op jit(solution)/shard_map/ppermute | solution.py:605
  1146.9 63.2 %collective-permute-start.33 = (bf16[1,384,1024]{2,1,0:T(8,128)(2,1)}, bf16[1,384,1024]{2,1,0:T(8,128)(2,1)}, u32[]{:S(2)}, u32[]{:S(2)}) collective-permute-start(bf16[1,384,1024]{2,1,0:T(8,128)(2,1)} %get-tuple-element.121), channel_id=1, source_target_pairs={{0,8},{2,10},{4,12},{6,14},{8,16},{10,18},{12,20},{14,22},{16,24},... | collective-permute-start | bytes 2359304 | tf_op jit(solution)/shard_map/ppermute | solution.py:605
  1161.2 58.4 %collective-permute-start.17 = (bf16[1,384,1024]{2,1,0:T(8,128)(2,1)}, bf16[1,384,1024]{2,1,0:T(8,128)(2,1)}, u32[]{:S(2)}, u32[]{:S(2)}) collective-permute-start(bf16[1,384,1024]{2,1,0:T(8,128)(2,1)} %get-tuple-element.125), channel_id=1, source_target_pairs={{0,8},{2,10},{4,12},{6,14},{8,16},{10,18},{12,20},{14,22},{16,24},... | collective-permute-start | bytes 2359304 | tf_op jit(solution)/shard_map/ppermute | solution.py:605
  1178.1 50.7 %collective-permute-start.70 = (bf16[1,384,1024]{2,1,0:T(8,128)(2,1)}, bf16[1,384,1024]{2,1,0:T(8,128)(2,1)}, u32[]{:S(2)}, u32[]{:S(2)}) collective-permute-start(bf16[1,384,1024]{2,1,0:T(8,128)(2,1)} %get-tuple-element.84), channel_id=1, source_target_pairs={{8,0},{10,2},{12,4},{14,6},{16,8},{18,10},{20,12},{22,14},{24,16},... | collective-permute-start | bytes 2359304 | tf_op jit(solution)/shard_map/ppermute | solution.py:605
  1210.1 52.2 %collective-permute-start.20 = (bf16[1,384,1024]{2,1,0:T(8,128)(2,1)S(1)}, bf16[1,384,1024]{2,1,0:T(8,128)(2,1)S(1)}, u32[]{:S(2)}, u32[]{:S(2)}) collective-permute-start(bf16[1,384,1024]{2,1,0:T(8,128)(2,1)S(1)} %add_convert_fusion.27), channel_id=1, source_target_pairs={{8,0},{10,2},{12,4},{14,6},{16,8},{18,10},{20,12},{22,14},{24,16},... | collective-permute-start | bytes 2359304 | tf_op jit(solution)/shard_map/ppermute | solution.py:605
  1211.9 52.4 %collective-permute-start.69 = (bf16[1,384,1024]{2,1,0:T(8,128)(2,1)}, bf16[1,384,1024]{2,1,0:T(8,128)(2,1)S(1)}, u32[]{:S(2)}, u32[]{:S(2)}) collective-permute-start(bf16[1,384,1024]{2,1,0:T(8,128)(2,1)} %get-tuple-element.84), channel_id=1, source_target_pairs={{0,8},{2,10},{4,12},{6,14},{8,16},{10,18},{12,20},{14,22},{16,24},... | collective-permute-start | bytes 2359304 | tf_op jit(solution)/shard_map/ppermute | solution.py:605
  1219.6 59.6 %collective-permute-start.38 = (bf16[1,384,1024]{2,1,0:T(8,128)(2,1)S(1)}, bf16[1,384,1024]{2,1,0:T(8,128)(2,1)S(1)}, u32[]{:S(2)}, u32[]{:S(2)}) collective-permute-start(bf16[1,384,1024]{2,1,0:T(8,128)(2,1)S(1)} %get-tuple-element.100), channel_id=1, source_target_pairs={{8,0},{10,2},{12,4},{14,6},{16,8},{18,10},{20,12},{22,14},{24,16},... | collective-permute-start | bytes 2359304 | tf_op jit(solution)/shard_map/ppermute | solution.py:605
  1228.7 67.3 %collective-permute-start.71 = (bf16[1,384,1024]{2,1,0:T(8,128)(2,1)}, bf16[1,384,1024]{2,1,0:T(8,128)(2,1)S(1)}, u32[]{:S(2)}, u32[]{:S(2)}) collective-permute-start(bf16[1,384,1024]{2,1,0:T(8,128)(2,1)} %collective-permute-done.70), channel_id=1, source_target_pairs={{8,0},{10,2},{12,4},{14,6},{16,8},{18,10},{20,12},{22,14},{24,16},... | collective-permute-start | bytes 2359304 | tf_op jit(solution)/shard_map/ppermute | solution.py:605
  1245.6 67.3 %collective-permute-start.55 = (bf16[1,384,1024]{2,1,0:T(8,128)(2,1)}, bf16[1,384,1024]{2,1,0:T(8,128)(2,1)S(1)}, u32[]{:S(2)}, u32[]{:S(2)}) collective-permute-start(bf16[1,384,1024]{2,1,0:T(8,128)(2,1)} %collective-permute-done.54), channel_id=1, source_target_pairs={{8,0},{10,2},{12,4},{14,6},{16,8},{18,10},{20,12},{22,14},{24,16},... | collective-permute-start | bytes 2359304 | tf_op jit(solution)/shard_map/ppermute | solution.py:605
  1262.3 54.3 %collective-permute-start.53 = (bf16[1,384,1024]{2,1,0:T(8,128)(2,1)}, bf16[1,384,1024]{2,1,0:T(8,128)(2,1)S(1)}, u32[]{:S(2)}, u32[]{:S(2)}) collective-permute-start(bf16[1,384,1024]{2,1,0:T(8,128)(2,1)} %get-tuple-element.92), channel_id=1, source_target_pairs={{0,8},{2,10},{4,12},{6,14},{8,16},{10,18},{12,20},{14,22},{16,24},... | collective-permute-start | bytes 2359304 | tf_op jit(solution)/shard_map/ppermute | solution.py:605
  1264.3 53.7 %collective-permute-start.37 = (bf16[1,384,1024]{2,1,0:T(8,128)(2,1)S(1)}, bf16[1,384,1024]{2,1,0:T(8,128)(2,1)S(1)}, u32[]{:S(2)}, u32[]{:S(2)}) collective-permute-start(bf16[1,384,1024]{2,1,0:T(8,128)(2,1)S(1)} %get-tuple-element.100), channel_id=1, source_target_pairs={{0,8},{2,10},{4,12},{6,14},{8,16},{10,18},{12,20},{14,22},{16,24},... | collective-permute-start | bytes 2359304 | tf_op jit(solution)/shard_map/ppermute | solution.py:605
  1279.2 50.6 %collective-permute-start.39 = (bf16[1,384,1024]{2,1,0:T(8,128)(2,1)S(1)}, bf16[1,384,1024]{2,1,0:T(8,128)(2,1)S(1)}, u32[]{:S(2)}, u32[]{:S(2)}) collective-permute-start(bf16[1,384,1024]{2,1,0:T(8,128)(2,1)S(1)} %collective-permute-done.38), channel_id=1, source_target_pairs={{8,0},{10,2},{12,4},{14,6},{16,8},{18,10},{20,12},{22,14},{24,16},... | collective-permute-start | bytes 2359304 | tf_op jit(solution)/shard_map/ppermute | solution.py:605
  1316.7 63.6 %collective-permute-start.22 = (bf16[1,384,1024]{2,1,0:T(8,128)(2,1)S(1)}, bf16[1,384,1024]{2,1,0:T(8,128)(2,1)S(1)}, u32[]{:S(2)}, u32[]{:S(2)}) collective-permute-start(bf16[1,384,1024]{2,1,0:T(8,128)(2,1)S(1)} %get-tuple-element.108), channel_id=1, source_target_pairs={{8,0},{10,2},{12,4},{14,6},{16,8},{18,10},{20,12},{22,14},{24,16},... | collective-permute-start | bytes 2359304 | tf_op jit(solution)/shard_map/ppermute | solution.py:605
  1318.0 64.3 %collective-permute-start.21 = (bf16[1,384,1024]{2,1,0:T(8,128)(2,1)S(1)}, bf16[1,384,1024]{2,1,0:T(8,128)(2,1)S(1)}, u32[]{:S(2)}, u32[]{:S(2)}) collective-permute-start(bf16[1,384,1024]{2,1,0:T(8,128)(2,1)S(1)} %get-tuple-element.108), channel_id=1, source_target_pairs={{0,8},{2,10},{4,12},{6,14},{8,16},{10,18},{12,20},{14,22},{16,24},... | collective-permute-start | bytes 2359304 | tf_op jit(solution)/shard_map/ppermute | solution.py:605
  1329.8 53.8 %collective-permute-start.73 = (bf16[1,384,1024]{2,1,0:T(8,128)(2,1)S(1)}, bf16[1,384,1024]{2,1,0:T(8,128)(2,1)S(1)}, u32[]{:S(2)}, u32[]{:S(2)}) collective-permute-start(bf16[1,384,1024]{2,1,0:T(8,128)(2,1)S(1)} %collective-permute-done.69), channel_id=1, source_target_pairs={{0,8},{2,10},{4,12},{6,14},{8,16},{10,18},{12,20},{14,22},{16,24},... | collective-permute-start | bytes 2359304 | tf_op jit(solution)/shard_map/ppermute | solution.py:605
  1397.2 323.2 %collective-permute-start.11 = (bf16[256,1024]{1,0:T(8,128)(2,1)}, bf16[256,1024]{1,0:T(8,128)(2,1)}, u32[]{:S(2)}, u32[]{:S(2)}) collective-permute-start(bf16[256,1024]{1,0:T(8,128)(2,1)} %convolution_convert_fusion.4), channel_id=1, source_target_pairs={{0,1},{1,0},{2,3},{3,2},{4,5},{5,4},{6,7},{7,6},{8,9},{9,8},{10,11... | collective-permute-start | bytes 1572872 | tf_op jit(solution)/shard_map/ppermute | solution.py:715
  1410.8 56.8 %collective-permute-start.42 = (bf16[1,384,1024]{2,1,0:T(8,128)(2,1)S(1)}, bf16[1,384,1024]{2,1,0:T(8,128)(2,1)S(1)}, u32[]{:S(2)}, u32[]{:S(2)}) collective-permute-start(bf16[1,384,1024]{2,1,0:T(8,128)(2,1)S(1)} %collective-permute-done.41), channel_id=1, source_target_pairs={{0,8},{2,10},{4,12},{6,14},{8,16},{10,18},{12,20},{14,22},{16,24},... | collective-permute-start | bytes 2359304 | tf_op jit(solution)/shard_map/ppermute | solution.py:605
  1417.0 55.4 %collective-permute-start.24 = (bf16[1,384,1024]{2,1,0:T(8,128)(2,1)S(1)}, bf16[1,384,1024]{2,1,0:T(8,128)(2,1)S(1)}, u32[]{:S(2)}, u32[]{:S(2)}) collective-permute-start(bf16[1,384,1024]{2,1,0:T(8,128)(2,1)S(1)} %collective-permute-done.23), channel_id=1, source_target_pairs={{8,0},{10,2},{12,4},{14,6},{16,8},{18,10},{20,12},{22,14},{24,16},... | collective-permute-start | bytes 2359304 | tf_op jit(solution)/shard_map/ppermute | solution.py:605
  1450.7 71.0 %collective-permute-start.75 = (bf16[4,384,1024]{2,1,0:T(8,128)(2,1)S(1)}, bf16[4,384,1024]{2,1,0:T(8,128)(2,1)S(1)}, u32[]{:S(2)}, u32[]{:S(2)}) collective-permute-start(bf16[4,384,1024]{2,1,0:T(8,128)(2,1)S(1)} %pad_maximum_fusion.3), channel_id=1, source_target_pairs={{0,4},{2,6},{4,0},{6,2},{8,12},{10,14},{12,8},{14,10},{16,20},{18,... | collective-permute-start | bytes 9437192 | tf_op jit(solution)/shard_map/ppermute | solution.py:605
  1467.6 121.7 %collective-permute-start.59 = (bf16[4,384,1024]{2,1,0:T(8,128)(2,1)}, bf16[4,384,1024]{2,1,0:T(8,128)(2,1)}, u32[]{:S(2)}, u32[]{:S(2)}) collective-permute-start(bf16[4,384,1024]{2,1,0:T(8,128)(2,1)} %pad_maximum_fusion.2), channel_id=1, source_target_pairs={{0,4},{2,6},{4,0},{6,2},{8,12},{10,14},{12,8},{14,10},{16,20},{18,... | collective-permute-start | bytes 9437192 | tf_op jit(solution)/shard_map/ppermute | solution.py:605
  1472.4 184.3 %collective-permute-start.43 = (bf16[4,384,1024]{2,1,0:T(8,128)(2,1)}, bf16[4,384,1024]{2,1,0:T(8,128)(2,1)}, u32[]{:S(2)}, u32[]{:S(2)}) collective-permute-start(bf16[4,384,1024]{2,1,0:T(8,128)(2,1)} %pad_maximum_fusion.1), channel_id=1, source_target_pairs={{0,4},{2,6},{4,0},{6,2},{8,12},{10,14},{12,8},{14,10},{16,20},{18,... | collective-permute-start | bytes 9437192 | tf_op jit(solution)/shard_map/ppermute | solution.py:605
  1481.0 231.0 %collective-permute-start.27 = (bf16[4,384,1024]{2,1,0:T(8,128)(2,1)}, bf16[4,384,1024]{2,1,0:T(8,128)(2,1)}, u32[]{:S(2)}, u32[]{:S(2)}) collective-permute-start(bf16[4,384,1024]{2,1,0:T(8,128)(2,1)} %pad_maximum_fusion), channel_id=1, source_target_pairs={{0,4},{2,6},{4,0},{6,2},{8,12},{10,14},{12,8},{14,10},{16,20},{18,... | collective-permute-start | bytes 9437192 | tf_op jit(solution)/shard_map/ppermute | solution.py:605
  1523.8 380.7 %collective-permute-start.76 = (bf16[8,384,1024]{2,1,0:T(8,128)(2,1)}, bf16[8,384,1024]{2,1,0:T(8,128)(2,1)}, u32[]{:S(2)}, u32[]{:S(2)}) collective-permute-start(bf16[8,384,1024]{2,1,0:T(8,128)(2,1)} %constant_dynamic-update-slice_fusion.15.mine_ref), channel_id=1, source_target_pairs={{0,2},{2,0},{4,6},{6,4},{8,10},{10,8},{12,14},{14,12},{16,18},{18,... | collective-permute-start | bytes 18874376 | tf_op jit(solution)/shard_map/ppermute | solution.py:605
  1593.2 329.3 %collective-permute-start.60 = (bf16[8,384,1024]{2,1,0:T(8,128)(2,1)}, bf16[8,384,1024]{2,1,0:T(8,128)(2,1)}, u32[]{:S(2)}, u32[]{:S(2)}) collective-permute-start(bf16[8,384,1024]{2,1,0:T(8,128)(2,1)} %constant_dynamic-update-slice_fusion.10.mine_ref), channel_id=1, source_target_pairs={{0,2},{2,0},{4,6},{6,4},{8,10},{10,8},{12,14},{14,12},{16,18},{18,... | collective-permute-start | bytes 18874376 | tf_op jit(solution)/shard_map/ppermute | solution.py:605
  1660.7 279.9 %collective-permute-start.44 = (bf16[8,384,1024]{2,1,0:T(8,128)(2,1)}, bf16[8,384,1024]{2,1,0:T(8,128)(2,1)}, u32[]{:S(2)}, u32[]{:S(2)}) collective-permute-start(bf16[8,384,1024]{2,1,0:T(8,128)(2,1)} %constant_dynamic-update-slice_fusion.5.mine_ref), channel_id=1, source_target_pairs={{0,2},{2,0},{4,6},{6,4},{8,10},{10,8},{12,14},{14,12},{16,18},{18,... | collective-permute-start | bytes 18874376 | tf_op jit(solution)/shard_map/ppermute | solution.py:605
  1715.8 242.9 %collective-permute-start.28 = (bf16[8,384,1024]{2,1,0:T(8,128)(2,1)}, bf16[8,384,1024]{2,1,0:T(8,128)(2,1)}, u32[]{:S(2)}, u32[]{:S(2)}) collective-permute-start(bf16[8,384,1024]{2,1,0:T(8,128)(2,1)} %constant_dynamic-update-slice_fusion.mine_ref), channel_id=1, source_target_pairs={{0,2},{2,0},{4,6},{6,4},{8,10},{10,8},{12,14},{14,12},{16,18},{18,... | collective-permute-start | bytes 18874376 | tf_op jit(solution)/shard_map/ppermute | solution.py:605
  1783.4 80.2 %collective-permute-start.8 = (bf16[1024,1024]{1,0:T(8,128)(2,1)}, bf16[1024,1024]{1,0:T(8,128)(2,1)S(1)}, u32[]{:S(2)}, u32[]{:S(2)}) collective-permute-start(bf16[1024,1024]{1,0:T(8,128)(2,1)} %fusion.27), channel_id=1, source_target_pairs={{0,1},{1,0},{2,3},{3,2},{4,5},{5,4},{6,7},{7,6},{8,9},{9,8},{10,11... | collective-permute-start | bytes 6291464 | tf_op jit(solution)/shard_map/ppermute | solution.py:715
  (122 other events, 3508.2 us)
Sparse Core Ops, SparseCore 0:
  1792.6 104.0 all-reduce.2
